TPU v7x, 128 devices: a whole 4x4x4 slice. The times are simulated.
128 devices in a mesh: shard: 8 (over y_lo, z), ctx: 4 (over x), tp: 4 (over y_hi, core).
Axes of the slice: x: 4, y: 4 (y_hi: 2, y_lo: 2; y = y_hi * 2 + y_lo), z: 4, core: 2. Of those that a mesh axis runs over, the one named last changes fastest.
Arguments:
- tokens: bfloat16 [16, 1376, 1024], P('shard', 'ctx'), may hold values from -6 to 6
- cotangent: bfloat16 [16, 1376, 1024], P('shard', 'ctx'), may hold values from -6 to 6
- slot_live: int32 [16], P('shard'), may hold values from 0 to 1, as said below
- block_rows: int32 [16, 4], P('shard'), may hold values from 1 to 344, 1370 in all within a row
- ln1_gain: float32 [1024], replicated, may hold values from 0.1 to 1.9
- ln1_bias: float32 [1024], replicated, may hold values from -3 to 3
- w_qkv: bfloat16 [1024, 3, 1024], P(('shard', 'ctx'), None, 'tp'), may hold values from -0.1875 to 0.1875
- b_qv: float32 [2, 1024], P(None, 'tp'), may hold values from -3 to 3
- w_proj: bfloat16 [1024, 1024], P(('shard', 'ctx'), 'tp'), may hold values from -1.5 to 1.5
- b_proj: float32 [1024], replicated, may hold values from -3 to 3
- scale_attn: float32 [1024], replicated, may hold values from 0.1 to 1.9
- ln2_gain: float32 [1024], replicated, may hold values from 0.1 to 1.9
- ln2_bias: float32 [1024], replicated, may hold values from -3 to 3
- w_up: bfloat16 [1024, 4096], P(('shard', 'ctx'), 'tp'), may hold values from -0.1875 to 0.1875
- b_up: float32 [4096], P('tp'), may hold values from -3 to 3
- w_down: bfloat16 [1024, 4096], P(('shard', 'ctx'), 'tp'), may hold values from -0.09375 to 0.09375
- b_down: float32 [1024], replicated, may hold values from -3 to 3
- scale_mlp: float32 [1024], replicated, may hold values from 0.1 to 1.9
Outputs:
- result: bfloat16 [16, 1376, 1024], P('shard', 'ctx')
- d_tokens: float32 [16, 1376, 1024], P('shard', 'ctx')
- d_ln1_gain: float32 [1024], replicated
- d_ln1_bias: float32 [1024], replicated
- d_w_qkv: float32 [1024, 3, 1024], P(('shard', 'ctx'), None, 'tp')
- d_b_qv: float32 [2, 1024], P(None, 'tp')
- d_w_proj: float32 [1024, 1024], P(('shard', 'ctx'), 'tp')
- d_b_proj: float32 [1024], replicated
- d_scale_attn: float32 [1024], replicated
- d_ln2_gain: float32 [1024], replicated
- d_ln2_bias: float32 [1024], replicated
- d_w_up: float32 [1024, 4096], P(('shard', 'ctx'), 'tp')
- d_b_up: float32 [4096], P('tp')
- d_w_down: float32 [1024, 4096], P(('shard', 'ctx'), 'tp')
- d_b_down: float32 [1024], replicated
- d_scale_mlp: float32 [1024], replicated
Inputs may be any that keep to these rules, and one draw needn't show every extreme that they name: `slot_live`: each index of shard owns 2 consecutive slots, the first of which always holds an image; exactly 13 slots hold one. `block_rows`: each slot's row of 4 entries sums to 1370.
All inputs are finite; a program needn't handle non-finite values.
Results may differ from a plain program's by a relative error of at most 0.02.
Values may be sent and summed in bfloat16 or wider, within the bound.
No kernel may reach another device: no remote copies, remote signals or barrier semaphores. Data moves between devices by JAX's collectives and lax.ppermute only.
A program may use at most 128 MiB of HBM per device.

v0:
```python
import jax
import jax.numpy as jnp
from jax import lax
from jax.sharding import PartitionSpec as P

HEAD_DIM = 64


EPSILON = 1e-06
MASKED = -1e30


def layer_stats(values):
    average = jnp.mean(values, axis=-1, keepdims=True)
    centered = values - average
    variance = jnp.mean(centered * centered, axis=-1, keepdims=True)
    inverse = lax.rsqrt(variance + EPSILON)
    return (centered * inverse, inverse)


def norm_back(grad_hat, normal_hat, inverse):
    first_term = jnp.mean(grad_hat, axis=-1, keepdims=True)
    second_term = jnp.mean(grad_hat * normal_hat, axis=-1, keepdims=True)
    return inverse * (grad_hat - first_term - normal_hat * second_term)


def tensor_sum(partial_rows):
    return lax.psum(partial_rows, "tp")


def input_sum(partial_rows):
    return lax.psum(partial_rows, "tp")


def attention_scores(queries, all_keys, key_valid, heads_dev):
    slot_count, block_len = (queries.shape[0], queries.shape[1])
    key_count = all_keys.shape[1]
    split_queries = queries.reshape(slot_count, block_len, heads_dev, HEAD_DIM)
    split_keys = all_keys.reshape(slot_count, key_count, heads_dev, HEAD_DIM)
    scores = jnp.einsum(
        "sqhe,skhe->shqk", split_queries, split_keys, preferred_element_type=jnp.float32
    ) * HEAD_DIM ** (-0.5)
    return jnp.where(key_valid[:, None, None, :], scores, MASKED)


def per_device(
    tokens,
    cotangent,
    slot_live,
    block_rows,
    ln1_gain,
    ln1_bias,
    w_qkv,
    b_qv,
    w_proj,
    b_proj,
    scale_attn,
    ln2_gain,
    ln2_bias,
    w_up,
    b_up,
    w_down,
    b_down,
    scale_mlp,
):
    slot_count, block_len, model_width = tokens.shape
    ctx_count = lax.axis_size("ctx")
    key_count = block_len * ctx_count
    heads_dev = w_qkv.shape[2] // HEAD_DIM
    head_width = heads_dev * HEAD_DIM
    positions = jnp.arange(key_count, dtype=jnp.int32)
    owners = positions // block_len
    within = positions % block_len
    matches = owners[:, None] == jnp.arange(ctx_count, dtype=jnp.int32)[None, :]
    counts_at = jnp.sum(jnp.where(matches[None], block_rows[:, None, :], 0), axis=-1)
    key_valid = (within[None, :] < counts_at) & (slot_live[:, None] > 0)
    row_valid = lax.dynamic_slice_in_dim(key_valid, lax.axis_index("ctx") * block_len, block_len, 1)
    row_mask = row_valid.astype(jnp.float32)[..., None]
    full_qkv, full_proj, full_up, full_down = (
        lax.all_gather(w_qkv, ("shard", "ctx"), axis=0, tiled=True),
        lax.all_gather(w_proj, ("shard", "ctx"), axis=0, tiled=True),
        lax.all_gather(w_up, ("shard", "ctx"), axis=0, tiled=True),
        lax.all_gather(w_down, ("shard", "ctx"), axis=0, tiled=True),
    )
    source = tokens.astype(jnp.float32)
    normal_one, inverse_one = layer_stats(source)
    normed = (normal_one * ln1_gain + ln1_bias).astype(jnp.bfloat16)
    shifts = jnp.stack([b_qv[0], jnp.zeros_like(b_qv[0]), b_qv[1]])
    mixed_qkv = (
        jnp.einsum("sbd,dcf->sbcf", normed, full_qkv, preferred_element_type=jnp.float32) + shifts
    ).astype(jnp.bfloat16)
    queries = mixed_qkv[:, :, 0]
    key_rows = mixed_qkv[:, :, 1]
    value_rows = mixed_qkv[:, :, 2]
    all_keys, all_values = (
        lax.all_gather(key_rows, "ctx", axis=1, tiled=True),
        lax.all_gather(value_rows, "ctx", axis=1, tiled=True),
    )
    scores = attention_scores(queries, all_keys, key_valid, heads_dev)
    top_score = jnp.max(scores, axis=-1, keepdims=True)
    exp_scores = jnp.exp(scores - top_score)
    denominator = jnp.sum(exp_scores, axis=-1, keepdims=True)
    log_total = top_score + jnp.log(denominator)
    soft_weights = (exp_scores / denominator).astype(jnp.bfloat16)
    split_values = all_values.reshape(slot_count, key_count, heads_dev, HEAD_DIM)
    attended = jnp.einsum(
        "shqk,skhe->sqhe", soft_weights, split_values, preferred_element_type=jnp.float32
    )
    attended = attended.reshape(slot_count, block_len, head_width).astype(jnp.bfloat16)
    attn_part = jnp.einsum("sbf,df->sbd", attended, full_proj, preferred_element_type=jnp.float32)
    branch_attn = tensor_sum(attn_part) + b_proj
    middle = source + scale_attn * branch_attn
    normal_two, inverse_two = layer_stats(middle)
    second_here = (normal_two * ln2_gain + ln2_bias).astype(jnp.bfloat16)
    hidden = (
        jnp.einsum("sbd,dh->sbh", second_here, full_up, preferred_element_type=jnp.float32) + b_up
    )
    active = jax.nn.gelu(hidden, approximate=False).astype(jnp.bfloat16)
    mlp_part = jnp.einsum("sbh,dh->sbd", active, full_down, preferred_element_type=jnp.float32)
    branch_mlp = tensor_sum(mlp_part) + b_down
    result_here = (row_mask * (middle + scale_mlp * branch_mlp)).astype(jnp.bfloat16)
    grad_out = row_mask * cotangent.astype(jnp.float32)
    grad_scale_mlp = jnp.sum(grad_out * branch_mlp, axis=(0, 1))
    grad_branch_mlp = (grad_out * scale_mlp).astype(jnp.bfloat16)
    grad_b_down = jnp.sum(grad_branch_mlp.astype(jnp.float32), axis=(0, 1))
    grad_w_down = jnp.einsum(
        "sbd,sbh->dh", grad_branch_mlp, active, preferred_element_type=jnp.float32
    )
    grad_active = jnp.einsum(
        "sbd,dh->sbh", grad_branch_mlp, full_down, preferred_element_type=jnp.float32
    )
    gelu_back = jax.vjp(lambda inside: jax.nn.gelu(inside, approximate=False), hidden)[1]
    grad_hidden = gelu_back(grad_active)[0].astype(jnp.bfloat16)
    grad_b_up = jnp.sum(grad_hidden.astype(jnp.float32), axis=(0, 1))
    grad_w_up = jnp.einsum(
        "sbd,sbh->dh", second_here, grad_hidden, preferred_element_type=jnp.float32
    )
    second_part = jnp.einsum(
        "sbh,dh->sbd", grad_hidden, full_up, preferred_element_type=jnp.float32
    )
    grad_second = input_sum(second_part)
    grad_ln2_gain = jnp.sum(grad_second * normal_two, axis=(0, 1))
    grad_ln2_bias = jnp.sum(grad_second, axis=(0, 1))
    grad_middle = grad_out + norm_back(grad_second * ln2_gain, normal_two, inverse_two)
    grad_scale_attn = jnp.sum(grad_middle * branch_attn, axis=(0, 1))
    grad_branch_here = (grad_middle * scale_attn).astype(jnp.bfloat16)
    grad_b_proj = jnp.sum(grad_branch_here.astype(jnp.float32), axis=(0, 1))
    grad_w_proj = jnp.einsum(
        "sbd,sbf->df", grad_branch_here, attended, preferred_element_type=jnp.float32
    )
    grad_attended = jnp.einsum(
        "sbd,df->sbf", grad_branch_here, full_proj, preferred_element_type=jnp.float32
    ).astype(jnp.bfloat16)
    split_grad = grad_attended.reshape(slot_count, block_len, heads_dev, HEAD_DIM)
    scores_again = attention_scores(queries, all_keys, key_valid, heads_dev)
    probs = jnp.exp(scores_again - log_total)
    split_keys = all_keys.reshape(slot_count, key_count, heads_dev, HEAD_DIM)
    split_queries = queries.reshape(slot_count, block_len, heads_dev, HEAD_DIM)
    grad_probs = jnp.einsum(
        "sqhe,skhe->shqk", split_grad, split_values, preferred_element_type=jnp.float32
    )
    row_dot = jnp.sum(probs * grad_probs, axis=-1, keepdims=True)
    grad_scores = (probs * (grad_probs - row_dot)).astype(jnp.bfloat16)
    grad_queries = jnp.einsum(
        "shqk,skhe->sqhe", grad_scores, split_keys, preferred_element_type=jnp.float32
    ) * HEAD_DIM ** (-0.5)
    grad_queries = grad_queries.reshape(slot_count, block_len, head_width).astype(jnp.bfloat16)
    probs_low = probs.astype(jnp.bfloat16)
    grad_values_part = jnp.einsum(
        "shqk,sqhe->skhe", probs_low, split_grad, preferred_element_type=jnp.float32
    )
    grad_keys_part = jnp.einsum(
        "shqk,sqhe->skhe", grad_scores, split_queries, preferred_element_type=jnp.float32
    ) * HEAD_DIM ** (-0.5)
    grad_keys, grad_values = (
        lax.psum_scatter(
            grad_keys_part.reshape(slot_count, key_count, head_width),
            "ctx",
            scatter_dimension=1,
            tiled=True,
        ),
        lax.psum_scatter(
            grad_values_part.reshape(slot_count, key_count, head_width),
            "ctx",
            scatter_dimension=1,
            tiled=True,
        ),
    )
    grad_keys = grad_keys.astype(jnp.bfloat16)
    grad_values = grad_values.astype(jnp.bfloat16)
    grad_mixed = jnp.stack([grad_queries, grad_keys, grad_values], axis=2)
    grad_b_qv = jnp.stack(
        [
            jnp.sum(grad_queries.astype(jnp.float32), axis=(0, 1)),
            jnp.sum(grad_values.astype(jnp.float32), axis=(0, 1)),
        ]
    )
    grad_w_qkv = jnp.einsum("sbd,sbcf->dcf", normed, grad_mixed, preferred_element_type=jnp.float32)
    normed_part = jnp.einsum(
        "sbcf,dcf->sbd", grad_mixed, full_qkv, preferred_element_type=jnp.float32
    )
    grad_normed = input_sum(normed_part)
    grad_ln1_gain = jnp.sum(grad_normed * normal_one, axis=(0, 1))
    grad_ln1_bias = jnp.sum(grad_normed, axis=(0, 1))
    tokens_here = grad_middle + norm_back(grad_normed * ln1_gain, normal_one, inverse_one)
    weight_parts = (
        lax.psum_scatter(grad_w_qkv, ("shard", "ctx"), scatter_dimension=0, tiled=True),
        lax.psum_scatter(grad_w_proj, ("shard", "ctx"), scatter_dimension=0, tiled=True),
        lax.psum_scatter(grad_w_up, ("shard", "ctx"), scatter_dimension=0, tiled=True),
        lax.psum_scatter(grad_w_down, ("shard", "ctx"), scatter_dimension=0, tiled=True),
    )
    small_parts = (
        lax.psum(grad_ln1_gain.astype(jnp.bfloat16), ("shard", "ctx")).astype(jnp.float32),
        lax.psum(grad_ln1_bias.astype(jnp.bfloat16), ("shard", "ctx")).astype(jnp.float32),
        lax.psum(grad_b_qv.astype(jnp.bfloat16), ("shard", "ctx")).astype(jnp.float32),
        lax.psum(grad_b_proj.astype(jnp.bfloat16), ("shard", "ctx")).astype(jnp.float32),
        lax.psum(grad_scale_attn.astype(jnp.bfloat16), ("shard", "ctx")).astype(jnp.float32),
        lax.psum(grad_ln2_gain.astype(jnp.bfloat16), ("shard", "ctx")).astype(jnp.float32),
        lax.psum(grad_ln2_bias.astype(jnp.bfloat16), ("shard", "ctx")).astype(jnp.float32),
        lax.psum(grad_b_up.astype(jnp.bfloat16), ("shard", "ctx")).astype(jnp.float32),
        lax.psum(grad_b_down.astype(jnp.bfloat16), ("shard", "ctx")).astype(jnp.float32),
        lax.psum(grad_scale_mlp.astype(jnp.bfloat16), ("shard", "ctx")).astype(jnp.float32),
    )
    return (
        result_here,
        tokens_here,
        small_parts[0],
        small_parts[1],
        weight_parts[0],
        small_parts[2],
        weight_parts[1],
        small_parts[3],
        small_parts[4],
        small_parts[5],
        small_parts[6],
        weight_parts[2],
        small_parts[7],
        weight_parts[3],
        small_parts[8],
        small_parts[9],
    )


def solution(mesh):
    placed = (
        P("shard", "ctx", None),
        P("shard", "ctx", None),
        P("shard"),
        P("shard", None),
        P(),
        P(),
        P(("shard", "ctx"), None, "tp"),
        P(None, "tp"),
        P(("shard", "ctx"), "tp"),
        P(),
        P(),
        P(),
        P(),
        P(("shard", "ctx"), "tp"),
        P("tp"),
        P(("shard", "ctx"), "tp"),
        P(),
        P(),
    )
    return jax.shard_map(
        per_device,
        mesh=mesh,
        in_specs=placed,
        out_specs=(
            P("shard", "ctx", None),
            P("shard", "ctx", None),
            P(),
            P(),
            P(("shard", "ctx"), None, "tp"),
            P(None, "tp"),
            P(("shard", "ctx"), "tp"),
            P(),
            P(),
            P(),
            P(),
            P(("shard", "ctx"), "tp"),
            P("tp"),
            P(("shard", "ctx"), "tp"),
            P(),
            P(),
        ),
        check_vma=False,
    )
```

profile of v0, /device:TPU:0, one launch (start us, length us, event | category | flops | bytes accessed | tf_op | source)
XLA Modules:
  0.0 1637.9 jit_solution(12294867799143030191)
XLA Ops:
  8.1 1.6 convert_reduce_fusion
  9.7 1.9 fusion.19
  11.7 153.0 %all-gather.8.cloned.1.call-done = bf16[1024,3,256]{2,0,1:T(8,128)(2,1)} async-done(((bf16[32,3,256]{2,0,1:T(8,128)(2,1)}), bf16[1024,3,256]{2,0,1:T(8,128)(2,1)}) %all-gather.8.cloned.1.call-update) | async-done | bytes 1572880 | tf_op jit(solution)/shard_map/all_gather | solution.py:80
  164.7 3.0 add_convert_fusion.2
  168.9 83.9 %all_gather.21 = bf16[1024,256]{1,0:T(8,128)(2,1)S(1)} all-gather(bf16[32,256]{1,0:T(8,128)(2,1)S(1)} %copy-done.44), channel_id=1, replica_groups=mesh['shard'=8,'ctx'=4,'tp'=4] {'shard','ctx'}, dimensions={0}, use_global_device_ids=true | all-gather | bytes 540672 | tf_op jit(solution)/shard_map/all_gather | solution.py:81
  253.3 1.8 copy.60
  255.1 7.9 fusion.64
  263.1 7.8 fusion
  270.9 3.4 all-gather.14.cloned.1.call-done
  274.3 1.8 copy.58
  276.1 7.5 fusion.43
  283.6 2.2 fusion.48
  287.3 69.8 %all-reduce.6.cloned.1.call-done = f32[2,344,1024]{2,1,0:T(8,128)} async-done(((f32[2,344,1024]{2,1,0:T(8,128)}), f32[2,344,1024]{2,1,0:T(8,128)}) %all-reduce.6.cloned.1.call-update) | async-done | bytes 2818064 | tf_op jit(solution)/shard_map/psum | solution.py:28
  357.2 2.7 fusion.61
  360.4 151.1 %all-gather.10.cloned.1.call-done = bf16[1024,1024]{1,0:T(8,128)(2,1)} async-done(((bf16[32,1024]{1,0:T(8,128)(2,1)}), bf16[1024,1024]{1,0:T(8,128)(2,1)}) %all-gather.10.cloned.1.call-update) | async-done | bytes 2097168 | tf_op jit(solution)/shard_map/all_gather | solution.py:82
  511.5 4.3 fusion.46
  515.8 1.6 copy-done.15
  517.3 7.5 multiply_convert_fusion.4
  524.9 141.5 %all-gather.12.cloned.1.call-done = bf16[1024,1024]{1,0:T(8,128)(2,1)} async-done(((bf16[32,1024]{1,0:T(8,128)(2,1)}), bf16[1024,1024]{1,0:T(8,128)(2,1)}) %all-gather.12.cloned.1.call-update) | async-done | bytes 2097168 | tf_op jit(solution)/shard_map/all_gather | solution.py:83
  666.3 7.1 fusion.66
  674.6 3.2 fusion.30
  678.1 70.6 %all-reduce.8.cloned.1.call-done = f32[2,344,1024]{2,1,0:T(8,128)} async-done(((f32[2,344,1024]{2,1,0:T(8,128)}), f32[2,344,1024]{2,1,0:T(8,128)}) %all-reduce.8.cloned.1.call-update) | async-done | bytes 2818064 | tf_op jit(solution)/shard_map/psum | solution.py:32
  748.7 3.9 multiply_reduce_fusion.2
  752.6 3.5 multiply_reduce_fusion.3
  756.0 1.6 copy-done.4
  761.3 8.5 fusion.2
  769.8 2.2 copy.64
  773.4 7.5 multiply_reduce_fusion
  780.9 7.3 multiply_convert_fusion
  788.2 3.9 convolution_multiply_fusion
  792.3 3.6 copy.63
  796.2 5.4 fusion.28
  801.7 3.7 fusion.65
  808.3 36.8 %reduce-scatter.7.cloned.1.call-done = f32[2,344,256]{2,1,0:T(8,128)} async-done(((f32[2,1376,256]{2,1,0:T(8,128)}), f32[2,344,256]{2,1,0:T(8,128)}) %reduce-scatter.7.cloned.1.call-update) | async-done | bytes 704528 | tf_op jit(solution)/shard_map/reduce_scatter | solution.py:176
  846.9 2.9 convolution_bitcast_fusion.3
  850.8 3.0 convolution_bitcast_fusion.4
  854.0 5.8 convolution_bitcast_fusion.1
  860.5 5.7 convolution_bitcast_fusion
  867.4 4.8 convolution_bitcast_fusion.2
  872.2 1.9 fusion.44
  875.5 90.8 %all-reduce.10.cloned.1.call-done = (f32[2,344,1024]{2,1,0:T(8,128)}, f32[2,344,1024]{2,1,0:T(8,128)}) async-done(((f32[2,344,1024]{2,1,0:T(8,128)}, f32[2,344,1024]{2,1,0:T(8,128)}), (f32[2,344,1024]{2,1,0:T(8,128)}, f32[2,344,1024]{2,1,0:T(8,128)})) %all-reduce.10.cloned.1.call-update) | async-done | bytes 5636112 | tf_op jit(solution)/shard_map/psum | solution.py:28
  966.3 3.8 fusion.18
  970.1 2.0 multiply_reduce_fusion.1
  972.1 157.4 %all-reduce.1 = (bf16[1024]{0:T(1024)(128)(2,1)S(1)}, bf16[1024]{0:T(1024)(128)(2,1)S(1)}, bf16[2,256]{1,0:T(2,128)(2,1)S(1)}, bf16[1024]{0:T(1024)(128)(2,1)S(1...) all-reduce(bf16[1024]{0:T(1024)(128)(2,1)S(1)} %get-tuple-element.1, ...), channel_id=1, replica_groups=mesh['shard'=8,'ctx'=4,'tp'=4] {'shard','ctx'}, use_global_device_ids=true, to_apply=%region_19.20 | all-reduce | flops 9728 | bytes 38912 | tf_op jit(solution)/shard_map/psum | solution.py:213
  1135.5 4.7 fusion.17
  1140.2 157.8 %reduce-scatter.15.cloned.1.call-done = f32[32,1024]{1,0:T(8,128)} async-done(((f32[1024,1024]{1,0:T(8,128)}), f32[32,1024]{1,0:T(8,128)}) %reduce-scatter.15.cloned.1.call-update) | async-done | bytes 131088 | tf_op jit(solution)/shard_map/reduce_scatter | solution.py:209
  1298.0 167.6 %reduce-scatter.17.cloned.1.call-done = f32[32,1024]{1,0:T(8,128)} async-done(((f32[1024,1024]{1,0:T(8,128)}), f32[32,1024]{1,0:T(8,128)}) %reduce-scatter.17.cloned.1.call-update) | async-done | bytes 131088 | tf_op jit(solution)/shard_map/reduce_scatter | solution.py:210
  1465.6 165.3 %reduce-scatter.11.cloned.1.call-done = f32[32,3,256]{2,0,1:T(8,128)} async-done(((f32[1024,3,256]{2,0,1:T(8,128)}), f32[32,3,256]{2,0,1:T(8,128)}) %reduce-scatter.11.cloned.1.call-update) | async-done | bytes 98320 | tf_op jit(solution)/shard_map/reduce_scatter | solution.py:207
  (201 shorter events, 26.5 us)
Async XLA Ops:
  7.2 157.5 %copy-start.3 = (bf16[2,344,1024]{2,1,0:T(8,128)(2,1)S(1)}, bf16[2,344,1024]{2,1,0:T(8,128)(2,1)}, u32[]{:S(2)}) copy-start(bf16[2,344,1024]{2,1,0:T(8,128)(2,1)} %param.18) | copy-start | bytes 4227076
  7.2 4.4 copy-start.53
  7.2 157.5 %copy-start.38 = (f32[1024]{0:T(1024)S(1)}, f32[1024]{0:T(1024)}, u32[]{:S(2)}) copy-start(f32[1024]{0:T(1024)} %param.22) | copy-start | bytes 12292
  7.2 157.5 %copy-start.59 = (f32[1024]{0:T(1024)S(1)}, f32[1024]{0:T(1024)}, u32[]{:S(2)}) copy-start(f32[1024]{0:T(1024)} %param.23) | copy-start | bytes 12292
  7.2 157.5 %all-gather.8.cloned.1.call-start = ((), (), s32[]{:S(2)}) async-start(), calls=%async_computation.6 | async-start | bytes 1622016 | tf_op jit(solution)/shard_map/all_gather | solution.py:80
  8.0 245.3 %all-gather.16.cloned.1.call-start = ((), (), s32[]{:S(2)}) async-start(), calls=%async_computation.18 | async-start | bytes 1761280 | tf_op jit(solution)/shard_map/all_gather | solution.py:96
  9.7 158.0 %copy-start.28 = (f32[2,344]{1,0:T(2,128)}, f32[2,344]{1,0:T(2,128)S(1)}, u32[]{:S(2)}) copy-start(f32[2,344]{1,0:T(2,128)S(1)} %broadcast_multiply_fusion.5) | copy-start | bytes 8260
  11.7 156.1 %copy-start.32 = (f32[2,344]{1,0:T(2,128)}, f32[2,344]{1,0:T(2,128)S(1)}, u32[]{:S(2)}) copy-start(f32[2,344]{1,0:T(2,128)S(1)} %add_rsqrt_fusion.1) | copy-start | bytes 8260
  11.7 157.1 %copy-start.54 = (s32[2,4]{1,0:T(2,128)S(1)}, s32[2,4]{1,0:T(2,128)}, u32[]{:S(2)}) copy-start(s32[2,4]{1,0:T(2,128)} %param.21) | copy-start | bytes 100
  11.7 157.2 %copy-start.44 = (bf16[32,256]{1,0:T(8,128)(2,1)S(1)}, bf16[32,256]{1,0:T(8,128)(2,1)}, u32[]{:S(2)}) copy-start(bf16[32,256]{1,0:T(8,128)(2,1)} %param.26) | copy-start | bytes 49156
  167.8 85.2 %copy-start.61 = (s32[2]{0:T(128)S(1)}, s32[2]{0:T(128)}, u32[]{:S(2)}) copy-start(s32[2]{0:T(128)} %param.20) | copy-start | bytes 28
  168.7 105.5 %all-gather.14.cloned.1.call-start = ((), (), s32[]{:S(2)}) async-start(), calls=%async_computation.17 | async-start | bytes 1761280 | tf_op jit(solution)/shard_map/all_gather | solution.py:97
  252.9 30.7 %copy-start.17 = (bf16[1024,256]{1,0:T(8,128)(2,1)}, bf16[1024,256]{1,0:T(8,128)(2,1)S(1)}, u32[]{:S(2)}) copy-start(bf16[1024,256]{1,0:T(8,128)(2,1)S(1)} %all_gather.21) | copy-start | bytes 1572868
  252.9 104.2 %all-reduce.6.cloned.1.call-start = ((), (), s32[]{:S(2)}) async-start(), calls=%async_computation.7 | async-start | bytes 5636096 | tf_op jit(solution)/shard_map/psum | solution.py:28
  255.1 7.9 copy-start.5
  276.1 7.5 copy-start.10
  283.6 73.6 %copy-start.36 = (f32[1024]{0:T(1024)S(1)}, f32[1024]{0:T(1024)}, u32[]{:S(2)}) copy-start(f32[1024]{0:T(1024)} %param.27) | copy-start | bytes 12292
  283.6 73.6 %copy-start.37 = (f32[1024]{0:T(1024)S(1)}, f32[1024]{0:T(1024)}, u32[]{:S(2)}) copy-start(f32[1024]{0:T(1024)} %param.28) | copy-start | bytes 12292
  285.8 225.6 %all-gather.10.cloned.1.call-start = ((), (), s32[]{:S(2)}) async-start(), calls=%async_computation.8 | async-start | bytes 2162688 | tf_op jit(solution)/shard_map/all_gather | solution.py:82
  286.4 379.9 %all-gather.12.cloned.1.call-start = ((), (), s32[]{:S(2)}) async-start(), calls=%async_computation.9 | async-start | bytes 2162688 | tf_op jit(solution)/shard_map/all_gather | solution.py:83
  287.0 461.6 %all-reduce.8.cloned.1.call-start = ((), (), s32[]{:S(2)}) async-start(), calls=%async_computation.10 | async-start | bytes 5636096 | tf_op jit(solution)/shard_map/psum | solution.py:32
  287.3 465.2 %copy-start.26 = (f32[2,344]{1,0:T(2,128)}, f32[2,344]{1,0:T(2,128)S(1)}, u32[]{:S(2)}) copy-start(f32[2,344]{1,0:T(2,128)S(1)} %dynamic-slice_convert_fusion) | copy-start | bytes 8260
  359.9 392.6 %copy-start.1 = (f32[2,344,1024]{2,1,0:T(8,128)}, f32[2,344,1024]{2,1,0:T(8,128)S(1)}, u32[]{:S(2)}) copy-start(f32[2,344,1024]{2,1,0:T(8,128)S(1)} %get-tuple-element.45) | copy-start | bytes 8454148
  359.9 151.6 %copy-start.40 = (f32[1024]{0:T(1024)S(1)}, f32[1024]{0:T(1024)}, u32[]{:S(2)}) copy-start(f32[1024]{0:T(1024)} %param.29) | copy-start | bytes 12292
  359.9 151.6 %copy-start.49 = (f32[1024]{0:T(1024)S(1)}, f32[1024]{0:T(1024)}, u32[]{:S(2)}) copy-start(f32[1024]{0:T(1024)} %param.32) | copy-start | bytes 12292
  359.9 151.6 %copy-start.57 = (f32[1024]{0:T(1024)S(1)}, f32[1024]{0:T(1024)}, u32[]{:S(2)}) copy-start(f32[1024]{0:T(1024)} %param.30) | copy-start | bytes 12292
  360.0 392.6 %copy-start.30 = (f32[2,344]{1,0:T(2,128)}, f32[2,344]{1,0:T(2,128)S(1)}, u32[]{:S(2)}) copy-start(f32[2,344]{1,0:T(2,128)S(1)} %broadcast_multiply_fusion.4) | copy-start | bytes 8260
  360.4 392.2 %copy-start.34 = (f32[2,344]{1,0:T(2,128)}, f32[2,344]{1,0:T(2,128)S(1)}, u32[]{:S(2)}) copy-start(f32[2,344]{1,0:T(2,128)S(1)} %add_rsqrt_fusion) | copy-start | bytes 8260
  517.3 149.0 %copy-start.42 = (f32[1024]{0:T(1024)S(1)}, f32[1024]{0:T(1024)}, u32[]{:S(2)}) copy-start(f32[1024]{0:T(1024)} %param.35) | copy-start | bytes 12292
  666.3 8.2 copy-start.55
  677.8 129.3 %reduce-scatter.9.cloned.1.call-start = ((), (), s32[]{:S(2)}) async-start(), calls=%async_computation.12 | async-start | bytes 3522560 | tf_op jit(solution)/shard_map/reduce_scatter | solution.py:182
  772.0 73.0 %reduce-scatter.7.cloned.1.call-start = ((), (), s32[]{:S(2)}) async-start(), calls=%async_computation.11 | async-start | bytes 3522560 | tf_op jit(solution)/shard_map/reduce_scatter | solution.py:176
  792.3 9.4 slice-start
  795.9 170.4 %all-reduce.10.cloned.1.call-start = ((), (), s32[]{:S(2)}) async-start(), calls=%async_computation.19 | async-start | bytes 11272192 | tf_op jit(solution)/shard_map/psum | solution.py:28
  796.2 5.4 slice-start.1
  796.2 5.4 copy-start.6
  805.3 41.6 %copy-start.56 = (bf16[1024,3,256]{2,0,1:T(8,128)(2,1)S(1)}, bf16[1024,3,256]{2,0,1:T(8,128)(2,1)}, u32[]{:S(2)}) copy-start(bf16[1024,3,256]{2,0,1:T(8,128)(2,1)} %all-gather.8.cloned.1.call-done) | copy-start | bytes 4718596
  806.6 43.2 %copy-start.21 = (bf16[2,344,1,256]{3,1,2,0:T(8,128)(2,1)}, bf16[2,344,1,256]{3,1,2,0:T(8,128)(2,1)S(1)}, u32[]{:S(2)}) copy-start(bf16[2,344,1,256]{3,1,2,0:T(8,128)(2,1)S(1)} %copy.65) | copy-start | bytes 1056772
  808.3 41.6 %copy-start.23 = (bf16[2,344,1,256]{3,1,2,0:T(8,128)(2,1)}, bf16[2,344,1,256]{3,1,2,0:T(8,128)(2,1)S(1)}, u32[]{:S(2)}) copy-start(bf16[2,344,1,256]{3,1,2,0:T(8,128)(2,1)S(1)} %convert_bitcast_fusion.1) | copy-start | bytes 1056772
  849.9 4.1 copy-start.2
  849.9 4.1 copy-start.31
  849.9 4.1 copy-start.35
  849.9 4.1 copy-start.41
  849.9 290.3 %reduce-scatter.13.cloned.1.call-start = ((), (), s32[]{:S(2)}) async-start(), calls=%async_computation.14 | async-start | bytes 1081344 | tf_op jit(solution)/shard_map/reduce_scatter | solution.py:208
  853.9 444.1 %reduce-scatter.15.cloned.1.call-start = ((), (), s32[]{:S(2)}) async-start(), calls=%async_computation.15 | async-start | bytes 4325376 | tf_op jit(solution)/shard_map/reduce_scatter | solution.py:209
  859.8 605.8 %reduce-scatter.17.cloned.1.call-start = ((), (), s32[]{:S(2)}) async-start(), calls=%async_computation.16 | async-start | bytes 4325376 | tf_op jit(solution)/shard_map/reduce_scatter | solution.py:210
  866.3 764.6 %reduce-scatter.11.cloned.1.call-start = ((), (), s32[]{:S(2)}) async-start(), calls=%async_computation.13 | async-start | bytes 3244032 | tf_op jit(solution)/shard_map/reduce_scatter | solution.py:207
  874.0 96.0 %copy-start.50 = (f32[1024]{0:T(1024)S(1)}, f32[1024]{0:T(1024)}, u32[]{:S(2)}) copy-start(f32[1024]{0:T(1024)} %param.34) | copy-start | bytes 12292
  (31 other events, 62.1 us)
Sparse Core Ops, SparseCore 0:
  9.7 154.9 all-gather.7
  168.8 26.0 all-gather.15
  253.0 21.1 all-gather.13
  286.0 71.1 all-reduce.5
  358.7 152.6 all-gather.9
  513.1 153.2 all-gather.11
  677.9 70.6 all-reduce.7
  772.2 34.9 reduce-scatter.8
  809.7 35.2 reduce-scatter.6
  850.0 116.2 all-reduce.9
  969.2 160.6 reduce-scatter.12
  1132.9 165.1 reduce-scatter.14
  1301.1 164.4 reduce-scatter.16
  1468.5 162.2 reduce-scatter.10
where the time goes:
time: 1650 us; the launch traced here: 1640 us
  waiting for transfers between devices  1210 us (73%)
  blocking collectives  241 us (15%)
  matrix products  86.9 us (5%)
  other arithmetic  59.4 us (4%)
  local copies, waits for them, and re-layouts  23.7 us (1%)
    reduce_scatter x1, waiting for transfers between devices, per_device(): lax.psum_scatter(grad_w_down, ('shard', 'ctx'), scatter_dimension=0, tile...  168 us
    reduce_scatter x1, waiting for transfers between devices, per_device(): lax.psum_scatter(grad_w_qkv, ('shard', 'ctx'), scatter_dimension=0, tiled...  165 us
    psum x2, waiting for transfers between devices, tensor_sum(): return lax.psum(partial_rows, 'tp')  161 us
    reduce_scatter x1, waiting for transfers between devices, per_device(): lax.psum_scatter(grad_w_up, ('shard', 'ctx'), scatter_dimension=0, tiled=...  158 us
    psum x1, blocking collectives, per_device(): lax.psum(grad_ln1_gain.astype(jnp.bfloat16), ('shard', 'ctx'))  157 us
    all_gather x1, waiting for transfers between devices, per_device(): lax.all_gather(w_qkv, ('shard', 'ctx'), axis=0, tiled=True)  153 us
    all_gather x1, waiting for transfers between devices, per_device(): lax.all_gather(w_up, ('shard', 'ctx'), axis=0, tiled=True)  151 us
    all_gather x1, waiting for transfers between devices, per_device(): lax.all_gather(w_down, ('shard', 'ctx'), axis=0, tiled=True)  141 us
  transfers between devices with their start and end apart: 14, of which 12 were waited for; matrix products, arithmetic and copies ran while one was open for 7% of the time, Pallas kernels for 0%

commit v1 on v0

v1 whole, which is shorter than its diff:
```python
import jax
import jax.numpy as jnp
from jax import lax
from jax.experimental import pallas as pl
from jax.experimental.pallas import tpu as pltpu
from jax.sharding import PartitionSpec as P

HEAD_DIM = 64
EPSILON = 1e-06
MASKED = -1e30
RING = 4
BF16 = jnp.bfloat16
F32 = jnp.float32

DIM = {"y": 0, "z": 1, "x": 2}


def shift_pairs(axis, step):
    if axis == "x":
        return "ctx", [(i, (i + step) % RING) for i in range(RING)]
    if axis == "z":
        return "shard", [
            (low * RING + z, low * RING + (z + step) % RING) for low in range(2) for z in range(RING)
        ]
    pairs = []
    for y in range(RING):
        for z in range(RING):
            for core in range(2):
                ends = [
                    ((at % 2) * RING + z) * 4 + (at // 2) * 2 + core for at in (y, (y + step) % RING)
                ]
                pairs.append(tuple(ends))
    return ("shard", "tp"), pairs


def shift(value, axis, step):
    names, pairs = shift_pairs(axis, step)
    return lax.ppermute(value, names, pairs)


def swap(value, bit):
    return lax.ppermute(value, "tp", [(i, i ^ bit) for i in range(4)])


def positions():
    shard, tp = lax.axis_index("shard"), lax.axis_index("tp")
    return {
        "x": lax.axis_index("ctx"),
        "z": shard % RING,
        "y": (tp // 2) * 2 + shard // RING,
    }


def assemble(parts, at, dim):
    shape = list(parts[0].shape)
    shape[dim] *= RING
    out = jnp.zeros(shape, parts[0].dtype)
    size = parts[0].shape[dim]
    for step, part in enumerate(parts):
        out = lax.dynamic_update_slice_in_dim(out, part, ((at - step) % RING) * size, dim)
    return out


def gather_axis(value, axis, at, dim):
    return assemble([value] + [shift(value, axis, s) for s in range(1, RING)], at, dim)


def gather(chunk, order, at):
    value = chunk[None, None, None]
    for axis in order:
        value = gather_axis(value, axis, at[axis], DIM[axis])
    return value.reshape(2, RING * RING * 2 * chunk.shape[0], chunk.shape[1])


def scatter_sum(halves, order, at):
    rows, columns = halves[0].shape
    value = jnp.stack(halves).reshape(RING, RING, RING, rows // 32, columns)
    for place, axis in enumerate(order):
        dim = DIM[axis]
        total = lax.dynamic_slice_in_dim(value, at[axis], 1, dim).astype(F32)
        for step in range(1, RING):
            block = lax.dynamic_slice_in_dim(value, (at[axis] + step) % RING, 1, dim)
            total = total + shift(block, axis, step).astype(F32)
        value = total if place == len(order) - 1 else total.astype(BF16)
    return value.reshape(rows // 32, columns)


def sum_everywhere(vector, at):
    for axis in ("x", "z", "y"):
        vector = jnp.sum(gather_axis(vector[None], axis, at[axis], 0), axis=0)
    return vector


def exchange(blocks, at):
    parts = [lax.dynamic_slice_in_dim(blocks, at, 1, 0)]
    for step in range(1, RING):
        parts.append(shift(lax.dynamic_slice_in_dim(blocks, (at + step) % RING, 1, 0), "x", step))
    return assemble(parts, at, 0)


def layer_stats(values):
    average = jnp.mean(values, axis=-1, keepdims=True)
    centered = values - average
    variance = jnp.mean(centered * centered, axis=-1, keepdims=True)
    inverse = lax.rsqrt(variance + EPSILON)
    return (centered * inverse, inverse)


def norm_back(grad_hat, normal_hat, inverse):
    first_term = jnp.mean(grad_hat, axis=-1, keepdims=True)
    second_term = jnp.mean(grad_hat * normal_hat, axis=-1, keepdims=True)
    return inverse * (grad_hat - first_term - normal_hat * second_term)


def dot(left, right, left_dim, right_dim):
    return lax.dot_general(
        left, right, (((left_dim,), (right_dim,)), ((), ())), preferred_element_type=F32
    )


def pair_sum(part):
    low = part.astype(BF16)
    return low.astype(F32) + swap(low, 1).astype(F32)


def attention_forward(q_ref, k_ref, v_ref, bias_ref, out_ref, log_ref):
    bias = bias_ref[...]
    for head in range(2):
        lanes = slice(head * HEAD_DIM, (head + 1) * HEAD_DIM)
        scaled = q_ref[:, lanes] * BF16(HEAD_DIM ** (-0.5))
        scores = dot(k_ref[:, lanes], scaled, 1, 1) + bias
        top = jnp.max(scores, axis=0, keepdims=True)
        powers = jnp.exp(scores - top)
        total = jnp.sum(powers, axis=0, keepdims=True)
        weights = (powers * (1.0 / total)).astype(BF16)
        mixed = dot(v_ref[:, lanes], weights, 0, 0)
        out_ref[:, lanes] = mixed.T.astype(BF16)
        log_ref[0, head : head + 1, :] = top + jnp.log(total)


def attention_backward(
    q_ref, k_ref, v_ref, g_ref, bias_ref, log_ref, dq_ref, dk_ref, dv_ref, dk_total, dv_total
):
    step = pl.program_id(0)

    @pl.when(step == 0)
    def _():
        dk_total[...] = jnp.zeros_like(dk_total)
        dv_total[...] = jnp.zeros_like(dv_total)

    bias = bias_ref[...]
    for head in range(2):
        lanes = slice(head * HEAD_DIM, (head + 1) * HEAD_DIM)
        scaled = q_ref[:, lanes] * BF16(HEAD_DIM ** (-0.5))
        keys, grad = k_ref[:, lanes], g_ref[:, lanes]
        scores = dot(keys, scaled, 1, 1) + bias
        probs = jnp.exp(scores - log_ref[0, head : head + 1, :])
        grad_probs = dot(v_ref[:, lanes], grad, 1, 1)
        row_dot = jnp.sum(probs * grad_probs, axis=0, keepdims=True)
        grad_scores = (probs * (grad_probs - row_dot)).astype(BF16)
        grad_q = dot(keys, grad_scores, 0, 0) * HEAD_DIM ** (-0.5)
        dq_ref[:, lanes] = grad_q.T.astype(BF16)
        dk_total[:, lanes] += dot(grad_scores, scaled, 1, 0)
        dv_total[:, lanes] += dot(probs.astype(BF16), grad, 1, 0)

    @pl.when(step == pl.num_programs(0) - 1)
    def _():
        dk_ref[...] = dk_total[...].astype(BF16)
        dv_ref[...] = dv_total[...].astype(BF16)


def attend(queries, keys, values, bias):
    rows, width = queries.shape
    block = rows // RING
    part = pl.BlockSpec((block, width), lambda i: (i, 0))
    whole = pl.BlockSpec((rows, width), lambda i: (0, 0))
    log_spec = pl.BlockSpec((1, 2, block), lambda i: (i, 0, 0))
    return pl.pallas_call(
        attention_forward,
        grid=(RING,),
        in_specs=[part, whole, whole, pl.BlockSpec((rows, 1), lambda i: (0, 0))],
        out_specs=[part, log_spec],
        out_shape=[
            jax.ShapeDtypeStruct((rows, width), BF16),
            jax.ShapeDtypeStruct((RING, 2, block), F32),
        ],
        compiler_params=pltpu.CompilerParams(vmem_limit_bytes=40 << 20),
        cost_estimate=pl.CostEstimate(
            flops=4 * rows * rows * width, bytes_accessed=8 * rows * width, transcendentals=2 * rows * rows
        ),
    )(queries, keys, values, bias)


def attend_back(queries, keys, values, grad, bias, logs):
    rows, width = queries.shape
    block = rows // RING
    part = pl.BlockSpec((block, width), lambda i: (i, 0))
    whole = pl.BlockSpec((rows, width), lambda i: (0, 0))
    log_spec = pl.BlockSpec((1, 2, block), lambda i: (i, 0, 0))
    return pl.pallas_call(
        attention_backward,
        grid=(RING,),
        in_specs=[part, whole, whole, part, pl.BlockSpec((rows, 1), lambda i: (0, 0)), log_spec],
        out_specs=[part, whole, whole],
        out_shape=[jax.ShapeDtypeStruct((rows, width), BF16)] * 3,
        scratch_shapes=[pltpu.VMEM((rows, width), F32)] * 2,
        compiler_params=pltpu.CompilerParams(vmem_limit_bytes=40 << 20),
        cost_estimate=pl.CostEstimate(
            flops=10 * rows * rows * width, bytes_accessed=14 * rows * width, transcendentals=2 * rows * rows
        ),
    )(queries, keys, values, grad, bias, logs)


def split_heads(blocks):
    return [blocks[j // 2][:, (j % 2) * 128 : (j % 2) * 128 + 128] for j in range(RING)]


def join_heads(four):
    return [jnp.concatenate([four[2 * h], four[2 * h + 1]], axis=1) for h in range(2)]


def both_slots(value, slot, core):
    half = value.shape[0] // 2
    sent = lax.dynamic_slice_in_dim(value, core * half, half, 0)
    mine = swap(sent, 2)
    other = swap(mine, 1)
    first, last = jnp.where(core == 0, mine, other), jnp.where(core == 0, other, mine)
    far = jnp.concatenate([first, last], axis=0)
    return jnp.stack([jnp.where(slot == 0, value, far), jnp.where(slot == 0, far, value)])


def per_device(
    tokens,
    cotangent,
    slot_live,
    block_rows,
    ln1_gain,
    ln1_bias,
    w_qkv,
    b_qv,
    w_proj,
    b_proj,
    scale_attn,
    ln2_gain,
    ln2_bias,
    w_up,
    b_up,
    w_down,
    b_down,
    scale_mlp,
):
    block_len = tokens.shape[1]
    at = positions()
    tp = lax.axis_index("tp")
    slot, core = tp // 2, tp % 2
    ctx = at["x"]

    orders = (("z", "y", "x"), ("x", "z", "y"), ("y", "x", "z"))
    full_qkv = [gather(w_qkv[:, c], orders[c], at) for c in range(3)]
    full_qkv, (w_up, w_down, w_proj) = lax.optimization_barrier((full_qkv, (w_up, w_down, w_proj)))
    full_proj = gather(w_proj, ("x", "z", "y"), at)
    full_up = gather(w_up, ("z", "y", "x"), at)
    full_down = gather(w_down, ("x", "y", "z"), at)
    biases = jnp.concatenate([b_qv.reshape(-1), b_up])
    other_biases = swap(biases, 2)
    biases = [jnp.where(slot == h, biases, other_biases) for h in range(2)]
    half_qv = b_qv.shape[1]

    counts = lax.dynamic_index_in_dim(block_rows, slot, 0, keepdims=False)
    live = lax.dynamic_index_in_dim(slot_live, slot, 0, keepdims=False) > 0
    within = jnp.arange(block_len, dtype=jnp.int32)
    key_valid = (within[None, :] < counts[:, None]) & live
    key_bias = jnp.where(key_valid, 0.0, MASKED).astype(F32).reshape(-1, 1)
    row_mask = (
        ((within < lax.dynamic_index_in_dim(counts, ctx, 0, keepdims=False)) & live)
        .astype(F32)[:, None]
    )

    source = lax.dynamic_index_in_dim(tokens, slot, 0, keepdims=False).astype(F32)
    normal_one, inverse_one = layer_stats(source)
    normed = (normal_one * ln1_gain + ln1_bias).astype(BF16)
    shifts = [
        [biases[h][:half_qv] for h in range(2)],
        None,
        [biases[h][half_qv : 2 * half_qv] for h in range(2)],
    ]
    mixed = []
    for c in range(3):
        columns = []
        for h in range(2):
            value = dot(normed, full_qkv[c][h], 1, 0)
            columns.append((value if shifts[c] is None else value + shifts[c][h]).astype(BF16))
        mixed.append(split_heads(columns))
    sent = jnp.stack([jnp.stack([mixed[c][j] for c in range(3)]) for j in range(RING)])
    heads = exchange(sent, ctx)
    queries, keys, values = (heads[:, c].reshape(RING * block_len, 128) for c in range(3))
    mixed_values, logs = attend(queries, keys, values, key_bias)
    attended = join_heads(exchange(mixed_values.reshape(RING, block_len, 128), ctx))
    attn_part = dot(attended[0], full_proj[0], 1, 1) + dot(attended[1], full_proj[1], 1, 1)
    branch_attn = pair_sum(attn_part) + b_proj
    middle = source + scale_attn * branch_attn

    normal_two, inverse_two = layer_stats(middle)
    second = (normal_two * ln2_gain + ln2_bias).astype(BF16)
    grad_out = row_mask * lax.dynamic_index_in_dim(cotangent, slot, 0, keepdims=False).astype(F32)
    grad_branch_mlp = (grad_out * scale_mlp).astype(BF16)
    grad_b_down = jnp.sum(grad_branch_mlp.astype(F32), axis=0)
    active, grad_hidden = [], []
    for h in range(2):
        hidden = dot(second, full_up[h], 1, 0) + biases[h][2 * half_qv :]
        below = 0.5 * (1.0 + lax.erf(hidden * 0.7071067811865476))
        slope = below + hidden * (jnp.exp(-0.5 * hidden * hidden) * 0.3989422804014327)
        active.append((hidden * below).astype(BF16))
        grad_active = dot(grad_branch_mlp, full_down[h], 1, 0)
        grad_hidden.append((grad_active * slope).astype(BF16))
    second_part = dot(grad_hidden[0], full_up[0], 1, 1) + dot(grad_hidden[1], full_up[1], 1, 1)
    grad_second = pair_sum(second_part)
    mlp_part = dot(active[0], full_down[0], 1, 1) + dot(active[1], full_down[1], 1, 1)
    branch_mlp = pair_sum(mlp_part) + b_down
    result_here = (row_mask * (middle + scale_mlp * branch_mlp)).astype(BF16)
    grad_scale_mlp = jnp.sum(grad_out * branch_mlp, axis=0)
    grad_b_up = [jnp.sum(grad_hidden[h].astype(F32), axis=0) for h in range(2)]
    grad_w_down = [dot(grad_branch_mlp, active[h], 0, 0).astype(BF16) for h in range(2)]
    grad_w_up = [dot(second, grad_hidden[h], 0, 0).astype(BF16) for h in range(2)]

    grad_ln2_gain = jnp.sum(grad_second * normal_two, axis=0)
    grad_ln2_bias = jnp.sum(grad_second, axis=0)
    grad_middle = grad_out + norm_back(grad_second * ln2_gain, normal_two, inverse_two)
    grad_scale_attn = jnp.sum(grad_middle * branch_attn, axis=0)
    grad_branch = (grad_middle * scale_attn).astype(BF16)
    grad_b_proj = jnp.sum(grad_branch.astype(F32), axis=0)
    grad_attended = [dot(grad_branch, full_proj[h], 1, 0).astype(BF16) for h in range(2)]
    grad_heads = exchange(jnp.stack(split_heads(grad_attended)), ctx).reshape(RING * block_len, 128)
    grad_w_proj = [dot(grad_branch, attended[h], 0, 0).astype(BF16) for h in range(2)]
    three = attend_back(queries, keys, values, grad_heads, key_bias, logs)
    returned = exchange(
        jnp.stack([value.reshape(RING, block_len, 128) for value in three], axis=1), ctx
    )
    grad_mixed = [join_heads(returned[:, c]) for c in range(3)]
    normed_part = sum(
        dot(grad_mixed[c][h], full_qkv[c][h], 1, 1) for c in range(3) for h in range(2)
    )
    grad_normed = pair_sum(normed_part)
    grad_ln1_gain = jnp.sum(grad_normed * normal_one, axis=0)
    grad_ln1_bias = jnp.sum(grad_normed, axis=0)
    tokens_here = grad_middle + norm_back(grad_normed * ln1_gain, normal_one, inverse_one)
    grad_w_qkv = [
        [dot(normed, grad_mixed[c][h], 0, 0).astype(BF16) for h in range(2)] for c in range(3)
    ]
    grad_b_qv = [
        jnp.sum(grad_mixed[c][h].astype(F32), axis=0) for h in range(2) for c in (0, 2)
    ]

    w_down_here = scatter_sum(grad_w_down, ("z", "y", "x"), at)
    w_up_here = scatter_sum(grad_w_up, ("x", "y", "z"), at)
    w_proj_here = scatter_sum(grad_w_proj, ("y", "z", "x"), at)
    w_qkv_here = jnp.stack(
        [scatter_sum(grad_w_qkv[c], orders[c][::-1], at) for c in range(3)], axis=1
    )
    wide = [
        grad_ln1_gain,
        grad_ln1_bias,
        grad_b_proj,
        grad_scale_attn,
        grad_ln2_gain,
        grad_ln2_bias,
        grad_b_down,
        grad_scale_mlp,
    ]
    vector = jnp.concatenate(wide + grad_b_qv + grad_b_up)
    vector = sum_everywhere(vector.reshape(-1, 128), at).reshape(-1)
    width = tokens.shape[2]
    sums = [vector[i * width : (i + 1) * width] for i in range(len(wide))]
    rest = vector[len(wide) * width :]
    qv_here = lax.dynamic_slice_in_dim(rest, slot * 2 * half_qv, 2 * half_qv, 0).reshape(2, half_qv)
    up_len = b_up.shape[0]
    up_here = lax.dynamic_slice_in_dim(rest, 4 * half_qv + slot * up_len, up_len, 0)
    result = both_slots(result_here, slot, core)
    d_tokens = both_slots(tokens_here.astype(BF16), slot, core).astype(F32)
    return (
        result,
        d_tokens,
        sums[0],
        sums[1],
        w_qkv_here,
        qv_here,
        w_proj_here,
        sums[2],
        sums[3],
        sums[4],
        sums[5],
        w_up_here,
        up_here,
        w_down_here,
        sums[6],
        sums[7],
    )


def solution(mesh):
    placed = (
        P("shard", "ctx", None),
        P("shard", "ctx", None),
        P("shard"),
        P("shard", None),
        P(),
        P(),
        P(("shard", "ctx"), None, "tp"),
        P(None, "tp"),
        P(("shard", "ctx"), "tp"),
        P(),
        P(),
        P(),
        P(),
        P(("shard", "ctx"), "tp"),
        P("tp"),
        P(("shard", "ctx"), "tp"),
        P(),
        P(),
    )
    return jax.shard_map(
        per_device,
        mesh=mesh,
        in_specs=placed,
        out_specs=(
            P("shard", "ctx", None),
            P("shard", "ctx", None),
            P(),
            P(),
            P(("shard", "ctx"), None, "tp"),
            P(None, "tp"),
            P(("shard", "ctx"), "tp"),
            P(),
            P(),
            P(),
            P(),
            P(("shard", "ctx"), "tp"),
            P("tp"),
            P(("shard", "ctx"), "tp"),
            P(),
            P(),
        ),
        check_vma=False,
    )
```

time: 1650 us -> 519 us (0.31)
  waiting for transfers between devices: 1210 us -> 247 us
  blocking collectives: 241 us -> 0 us
  starting transfers between devices: 1.5 us -> 164 us
  matrix products: 86.9 us -> 24.1 us
  other arithmetic: 59.4 us -> 28.3 us
  Pallas kernels: 0 us -> 24.1 us
    reduce_scatter x6 -> x0, waiting for transfers between devices: 528 us -> none  [the longest x1 168 us: per_device(): lax.psum_scatter(grad_w_down, ('shard', 'ctx'), scatter_dimension=0, tile...]
    all_gather x5 -> x0, waiting for transfers between devices: 449 us -> none  [the longest x1 153 us: per_device(): lax.all_gather(w_qkv, ('shard', 'ctx'), axis=0, tiled=True)]
    ppermute x0 -> x138, waiting for transfers between devices: none -> 247 us  [the longest x129 247 us: shift(): return lax.ppermute(value, names, pairs)]
    psum x3 -> x0, waiting for transfers between devices: 231 us -> none  [the longest x2 161 us: tensor_sum(): return lax.psum(partial_rows, 'tp')]
    ppermute x0 -> x138, starting transfers between devices: none -> 164 us  [the longest x129 156 us: shift(): return lax.ppermute(value, names, pairs)]
    psum x1 -> x0, blocking collectives: 157 us -> none  [per_device(): lax.psum(grad_ln1_gain.astype(jnp.bfloat16), ('shard', 'ctx'))]
    all_gather x1 -> x0, blocking collectives: 83.9 us -> none  [per_device(): lax.all_gather(w_proj, ('shard', 'ctx'), axis=0, tiled=True)]
    dot_general x18 -> x36, matrix products: 86.9 us -> 24.1 us  [dot(): lax.dot_general(left, right, (((left_dim,), (right_dim,)), ((), ())), pre...]
  transfers between devices with their start and end apart: 14 -> 138, of which waited for: 12 -> 51; matrix products, arithmetic and copies ran while one was open for 7% -> 11% of each run, Pallas kernels for 0% -> 5%
where the time goes in v1:
time: 519 us; the launch traced here: 510 us
  waiting for transfers between devices  247 us (48%)
  starting transfers between devices  164 us (32%)
  other arithmetic  28.3 us (5%)
  matrix products  24.1 us (5%)
  Pallas kernels  24.1 us (5%)
  local copies, waits for them, and re-layouts  19 us (4%)
    ppermute x129, waiting for transfers between devices, shift(): return lax.ppermute(value, names, pairs)  247 us
    ppermute x129, starting transfers between devices, shift(): return lax.ppermute(value, names, pairs)  156 us
    dot_general x36, matrix products, dot(): lax.dot_general(left, right, (((left_dim,), (right_dim,)), ((), ())), pre...  24.1 us
    pallas_call x1, Pallas kernels, attend_back(): pl.pallas_call(attention_backward, grid=(RING,), in_specs=[part, whole, w...  14.5 us
  transfers between devices with their start and end apart: 138, of which 51 were waited for; matrix products, arithmetic and copies ran while one was open for 11% of the time, Pallas kernels for 5%

profile of v1, /device:TPU:0, one launch (start us, length us, event | category | flops | bytes accessed | tf_op | source)
XLA Modules:
  0.0 510.2 jit_solution(8395927293345205160)
XLA Ops:
  3.6 3.6 collective-permute-start.1
  9.5 3.2 collective-permute-start.27
  20.6 2.8 collective-permute-start.10
  31.5 2.6 collective-permute-start.5
  49.6 3.7 collective-permute-done.6
  59.8 5.1 collective-permute-done.24
  67.3 2.8 collective-permute-start.36
  79.4 2.8 collective-permute-start.54
  86.1 2.7 collective-permute-start.30
  91.4 2.9 collective-permute-done.37
  103.3 9.6 %shard_map.297 = (bf16[1376,128]{1,0:T(8,128)(2,1)S(1)}, f32[4,2,344]{2,1,0:T(2,128)S(1)}) custom-call(bf16[1376,128]{1,0:T(8,128)(2,1)S(1)} %bitcast.357, bf16[1376,128]{1,0:T(8,128)(2,1)S(1)} %bitcast.355, bf16[1376,128]{1,0:T(8,128)(2,1)S(1)} %bitcast.353, f32[1376,1]{1,0:T(8,128)S(1)} %select_n.793.bias_ref), custom_call_target="tpu_custom_call" | custom-call | flops 969408512 | bytes 1409024 | tf_op jit(solution)/shard_map/pallas_call | solution.py:178
  113.0 3.9 collective-permute-start.41
  121.2 3.8 collective-permute-done.41
  128.1 5.4 %collective-permute-done.31 = bf16[1,344,128]{2,1,0:T(8,128)(2,1)S(1)} collective-permute-done((bf16[1,344,128]{2,1,0:T(8,128)(2,1)S(1)}, bf16[1,344,128]{2,1,0:T(8,128)(2,1)S(1)}, u32[]{:S(2)}, u32[]{:S(2)}) %collective-permute-start.31) | collective-permute-done | bytes 88096 | tf_op jit(solution)/shard_map/ppermute | solution.py:38
  133.6 6.0 %collective-permute-done.32 = bf16[1,344,128]{2,1,0:T(8,128)(2,1)S(1)} collective-permute-done((bf16[1,344,128]{2,1,0:T(8,128)(2,1)S(1)}, bf16[1,344,128]{2,1,0:T(8,128)(2,1)S(1)}, u32[]{:S(2)}, u32[]{:S(2)}) %collective-permute-start.32) | collective-permute-done | bytes 88096 | tf_op jit(solution)/shard_map/ppermute | solution.py:38
  139.6 4.5 collective-permute-done.33
  145.2 2.7 collective-permute-start.51
  154.5 39.9 %collective-permute-done.50 = bf16[4,4,1,32,1024]{4,3,2,1,0:T(8,128)(2,1)S(1)} collective-permute-done((bf16[4,4,1,32,1024]{4,3,2,1,0:T(8,128)(2,1)S(1)}, bf16[4,4,1,32,1024]{4,3,2,1,0:T(8,128)(2,1)S(1)}, u32[]{:S(2)}, u32[]{:S(2)}) %collective-permute-start.50) | collective-permute-done | bytes 1048608 | tf_op jit(solution)/shard_map/ppermute | solution.py:38
  198.0 21.3 %collective-permute-done.61 = bf16[4,1,4,32,1024]{4,3,2,1,0:T(8,128)(2,1)S(1)} collective-permute-done((bf16[4,1,4,32,1024]{4,3,2,1,0:T(8,128)(2,1)S(1)}, bf16[4,1,4,32,1024]{4,3,2,1,0:T(8,128)(2,1)S(1)}, u32[]{:S(2)}, u32[]{:S(2)}) %collective-permute-start.61) | collective-permute-done | bytes 1048608 | tf_op jit(solution)/shard_map/ppermute | solution.py:38
  239.5 2.9 fusion.22
  244.6 2.7 collective-permute-start.113
  251.1 3.6 collective-permute-done.66
  255.6 3.2 collective-permute-done.113
  263.8 40.6 %collective-permute-done.67 = bf16[1,344,128]{2,1,0:T(8,128)(2,1)S(1)} collective-permute-done((bf16[1,344,128]{2,1,0:T(8,128)(2,1)S(1)}, bf16[1,344,128]{2,1,0:T(8,128)(2,1)S(1)}, u32[]{:S(2)}, u32[]{:S(2)}) %collective-permute-start.67) | collective-permute-done | bytes 88096 | tf_op jit(solution)/shard_map/ppermute | solution.py:38
  304.5 2.7 collective-permute-start.116
  309.7 3.4 collective-permute-done.115
  313.4 13.8 %collective-permute-done.114 = bf16[1,1,4,32,256]{4,3,2,1,0:T(8,128)(2,1)S(1)} collective-permute-done((bf16[1,1,4,32,256]{4,3,2,1,0:T(8,128)(2,1)S(1)}, bf16[1,1,4,32,256]{4,3,2,1,0:T(8,128)(2,1)S(1)}, u32[]{:S(2)}, u32[]{:S(2)}) %collective-permute-start.114) | collective-permute-done | bytes 65568 | tf_op jit(solution)/shard_map/ppermute | solution.py:38
  327.2 14.5 %shard_map.298 = (bf16[1376,128]{1,0:T(8,128)(2,1)S(1)}, bf16[1376,128]{1,0:T(8,128)(2,1)S(1)}, bf16[1376,128]{1,0:T(8,128)(2,1)S(1)}) custom-call(bf16[1376,128]{1,0:T(8,128)(2,1)S(1)} %bitcast.358, bf16[1376,128]{1,0:T(8,128)(2,1)S(1)} %bitcast.356, bf16[1376,128]{1,0:T(8,128)(2,1)S(1)} %bitcast.354, bf16[1376,128]{1,0:T(8,128)(2,1)S(1)} %bitcast.352, ...), custom_call_target="tpu_custom_call" | custom-call | flops 2423521280 | bytes 2465792 | tf_op jit(solution)/shard_map/pallas_call | solution.py:200
  342.2 2.5 collective-permute-start.63
  344.7 2.5 add_convert_fusion.1
  347.1 3.3 collective-permute-start.119
  350.5 10.2 %collective-permute-done.129 = bf16[4,1,4,32,1024]{4,3,2,1,0:T(8,128)(2,1)} collective-permute-done((bf16[4,1,4,32,1024]{4,3,2,1,0:T(8,128)(2,1)S(1)}, bf16[4,1,4,32,1024]{4,3,2,1,0:T(8,128)(2,1)}, u32[]{:S(2)}, u32[]{:S(2)}) %collective-permute-start.129) | collective-permute-done | bytes 1048608 | tf_op jit(solution)/shard_map/ppermute | solution.py:38
  360.6 2.8 add_convert_fusion
  364.0 2.9 collective-permute-start.71
  366.9 2.9 collective-permute-start.125
  374.9 2.9 collective-permute-start.134
  381.8 6.4 %collective-permute-done.123 = bf16[1,4,1,32,1024]{4,3,2,1,0:T(8,128)(2,1)S(1)} collective-permute-done((bf16[1,4,1,32,1024]{4,3,2,1,0:T(8,128)(2,1)S(1)}, bf16[1,4,1,32,1024]{4,3,2,1,0:T(8,128)(2,1)S(1)}, u32[]{:S(2)}, u32[]{:S(2)}) %collective-permute-start.123) | collective-permute-done | bytes 262176 | tf_op jit(solution)/shard_map/ppermute | solution.py:38
  399.7 2.5 collective-permute-done.136
  423.2 9.3 %collective-permute-done.78 = f32[1,88,128]{2,1,0:T(8,128)S(1)} collective-permute-done((f32[1,88,128]{2,1,0:T(8,128)S(1)}, f32[1,88,128]{2,1,0:T(8,128)S(1)}, u32[]{:S(2)}, u32[]{:S(2)}) %collective-permute-start.78) | collective-permute-done | bytes 45088 | tf_op jit(solution)/shard_map/ppermute | solution.py:38
  433.3 4.7 collective-permute-done.79
  438.7 3.4 collective-permute-done.80
  442.8 4.7 collective-permute-done.81
  449.2 3.8 collective-permute-done.82
  453.5 4.1 collective-permute-done.83
  457.6 4.0 collective-permute-start.95
  488.1 2.8 collective-permute-start.110
  496.8 2.8 collective-permute-start.92
  502.3 2.7 collective-permute-done.91
  (561 shorter events, 208.5 us)
Async XLA Ops:
  1.6 21.9 %collective-permute-start = (bf16[1,1,1,32,256]{4,3,2,1,0:T(8,128)(2,1)S(1)}, bf16[1,1,1,32,256]{4,3,2,1,0:T(8,128)(2,1)S(1)}, u32[]{:S(2)}, u32[]{:S(2)}) collective-permute-start(bf16[1,1,1,32,256]{4,3,2,1,0:T(8,128)(2,1)S(1)} %get-tuple-element.177), channel_id=1, source_target_pairs={{0,16},{16,32},{32,48},{48,0},{64,80},{80,96},{96,112},{112,64},{1... | collective-permute-start | bytes 49160 | tf_op jit(solution)/shard_map/ppermute | solution.py:38
  3.6 21.4 %collective-permute-start.1 = (bf16[1,1,1,32,256]{4,3,2,1,0:T(8,128)(2,1)S(1)}, bf16[1,1,1,32,256]{4,3,2,1,0:T(8,128)(2,1)S(1)}, u32[]{:S(2)}, u32[]{:S(2)}) collective-permute-start(bf16[1,1,1,32,256]{4,3,2,1,0:T(8,128)(2,1)S(1)} %get-tuple-element.177), channel_id=1, source_target_pairs={{0,32},{16,48},{32,0},{48,16},{64,96},{80,112},{96,64},{112,80},{1... | collective-permute-start | bytes 49160 | tf_op jit(solution)/shard_map/ppermute | solution.py:38
  7.1 18.5 %collective-permute-start.2 = (bf16[1,1,1,32,256]{4,3,2,1,0:T(8,128)(2,1)S(1)}, bf16[1,1,1,32,256]{4,3,2,1,0:T(8,128)(2,1)S(1)}, u32[]{:S(2)}, u32[]{:S(2)}) collective-permute-start(bf16[1,1,1,32,256]{4,3,2,1,0:T(8,128)(2,1)S(1)} %get-tuple-element.177), channel_id=1, source_target_pairs={{0,48},{16,0},{32,16},{48,32},{64,112},{80,64},{96,80},{112,96},{1... | collective-permute-start | bytes 49160 | tf_op jit(solution)/shard_map/ppermute | solution.py:38
  12.7 14.8 %collective-permute-start.9 = (bf16[1,1,1,32,256]{4,3,2,1,0:T(8,128)(2,1)S(1)}, bf16[1,1,1,32,256]{4,3,2,1,0:T(8,128)(2,1)S(1)}, u32[]{:S(2)}, u32[]{:S(2)}) collective-permute-start(bf16[1,1,1,32,256]{4,3,2,1,0:T(8,128)(2,1)S(1)} %get-tuple-element.178), channel_id=1, source_target_pairs={{0,4},{4,8},{8,12},{12,0},{1,5},{5,9},{9,13},{13,1},{2,6},{6,10},{... | collective-permute-start | bytes 49160 | tf_op jit(solution)/shard_map/ppermute | solution.py:38
  65.9 12.1 %collective-permute-start.34 = (bf16[1,1,1,32,256]{4,3,2,1,0:T(8,128)(2,1)S(1)}, bf16[1,1,1,32,256]{4,3,2,1,0:T(8,128)(2,1)S(1)}, u32[]{:S(2)}, u32[]{:S(2)}) collective-permute-start(bf16[1,1,1,32,256]{4,3,2,1,0:T(8,128)(2,1)S(1)} %bitcast.413), channel_id=1, source_target_pairs={{0,4},{4,8},{8,12},{12,0},{1,5},{5,9},{9,13},{13,1},{2,6},{6,10},{... | collective-permute-start | bytes 49160 | tf_op jit(solution)/shard_map/ppermute | solution.py:38
  67.3 12.1 %collective-permute-start.36 = (bf16[1,1,1,32,256]{4,3,2,1,0:T(8,128)(2,1)S(1)}, bf16[1,1,1,32,256]{4,3,2,1,0:T(8,128)(2,1)S(1)}, u32[]{:S(2)}, u32[]{:S(2)}) collective-permute-start(bf16[1,1,1,32,256]{4,3,2,1,0:T(8,128)(2,1)S(1)} %bitcast.415), channel_id=1, source_target_pairs={{0,12},{4,0},{8,4},{12,8},{1,13},{5,1},{9,5},{13,9},{2,14},{6,2},{... | collective-permute-start | bytes 49160 | tf_op jit(solution)/shard_map/ppermute | solution.py:38
  83.0 17.2 %collective-permute-start.28 = (bf16[1,3,344,128]{3,2,1,0:T(8,128)(2,1)S(1)}, bf16[1,3,344,128]{3,2,1,0:T(8,128)(2,1)S(1)}, u32[]{:S(2)}, u32[]{:S(2)}) collective-permute-start(bf16[1,3,344,128]{3,2,1,0:T(8,128)(2,1)S(1)} %get-tuple-element.93), channel_id=1, source_target_pairs={{0,4},{4,8},{8,12},{12,0},{1,5},{5,9},{9,13},{13,1},{2,6},{6,10},{... | collective-permute-start | bytes 792584 | tf_op jit(solution)/shard_map/ppermute | solution.py:38
  84.4 17.2 %collective-permute-start.29 = (bf16[1,3,344,128]{3,2,1,0:T(8,128)(2,1)S(1)}, bf16[1,3,344,128]{3,2,1,0:T(8,128)(2,1)S(1)}, u32[]{:S(2)}, u32[]{:S(2)}) collective-permute-start(bf16[1,3,344,128]{3,2,1,0:T(8,128)(2,1)S(1)} %get-tuple-element.92), channel_id=1, source_target_pairs={{0,8},{4,12},{8,0},{12,4},{1,9},{5,13},{9,1},{13,5},{2,10},{6,14},... | collective-permute-start | bytes 792584 | tf_op jit(solution)/shard_map/ppermute | solution.py:38
  86.1 16.4 %collective-permute-start.30 = (bf16[1,3,344,128]{3,2,1,0:T(8,128)(2,1)S(1)}, bf16[1,3,344,128]{3,2,1,0:T(8,128)(2,1)S(1)}, u32[]{:S(2)}, u32[]{:S(2)}) collective-permute-start(bf16[1,3,344,128]{3,2,1,0:T(8,128)(2,1)S(1)} %get-tuple-element.91), channel_id=1, source_target_pairs={{0,12},{4,0},{8,4},{12,8},{1,13},{5,1},{9,5},{13,9},{2,14},{6,2},{... | collective-permute-start | bytes 792584 | tf_op jit(solution)/shard_map/ppermute | solution.py:38
  95.4 17.7 %collective-permute-start.47 = (bf16[1,4,1,32,1024]{4,3,2,1,0:T(8,128)(2,1)S(1)}, bf16[1,4,1,32,1024]{4,3,2,1,0:T(8,128)(2,1)S(1)}, u32[]{:S(2)}, u32[]{:S(2)}) collective-permute-start(bf16[1,4,1,32,1024]{4,3,2,1,0:T(8,128)(2,1)S(1)} %constant_dynamic-update-slice_fusion.38), channel_id=1, source_target_pairs={{0,64},{1,65},{16,80},{17,81},{32,96},{33,97},{48,112},{49,113},{6... | collective-permute-start | bytes 786440 | tf_op jit(solution)/shard_map/ppermute | solution.py:38
  98.6 18.4 %collective-permute-start.48 = (bf16[1,4,1,32,1024]{4,3,2,1,0:T(8,128)(2,1)S(1)}, bf16[1,4,1,32,1024]{4,3,2,1,0:T(8,128)(2,1)S(1)}, u32[]{:S(2)}, u32[]{:S(2)}) collective-permute-start(bf16[1,4,1,32,1024]{4,3,2,1,0:T(8,128)(2,1)S(1)} %constant_dynamic-update-slice_fusion.38), channel_id=1, source_target_pairs={{0,2},{1,3},{16,18},{17,19},{32,34},{33,35},{48,50},{49,51},{64,66... | collective-permute-start | bytes 786440 | tf_op jit(solution)/shard_map/ppermute | solution.py:38
  100.2 44.9 %collective-permute-start.49 = (bf16[1,4,1,32,1024]{4,3,2,1,0:T(8,128)(2,1)S(1)}, bf16[1,4,1,32,1024]{4,3,2,1,0:T(8,128)(2,1)S(1)}, u32[]{:S(2)}, u32[]{:S(2)}) collective-permute-start(bf16[1,4,1,32,1024]{4,3,2,1,0:T(8,128)(2,1)S(1)} %constant_dynamic-update-slice_fusion.38), channel_id=1, source_target_pairs={{0,66},{1,67},{16,82},{17,83},{32,98},{33,99},{48,114},{49,115},{6... | collective-permute-start | bytes 786440 | tf_op jit(solution)/shard_map/ppermute | solution.py:38
  101.7 43.5 %collective-permute-start.56 = (bf16[1,1,4,32,1024]{4,3,2,1,0:T(8,128)(2,1)S(1)}, bf16[1,1,4,32,1024]{4,3,2,1,0:T(8,128)(2,1)S(1)}, u32[]{:S(2)}, u32[]{:S(2)}) collective-permute-start(bf16[1,1,4,32,1024]{4,3,2,1,0:T(8,128)(2,1)S(1)} %constant_dynamic-update-slice_fusion.26), channel_id=1, source_target_pairs={{0,64},{1,65},{16,80},{17,81},{32,96},{33,97},{48,112},{49,113},{6... | collective-permute-start | bytes 786440 | tf_op jit(solution)/shard_map/ppermute | solution.py:38
  102.4 17.3 %collective-permute-start.40 = (bf16[1,4,4,32,256]{4,3,2,1,0:T(8,128)(2,1)S(1)}, bf16[1,4,4,32,256]{4,3,2,1,0:T(8,128)(2,1)S(1)}, u32[]{:S(2)}, u32[]{:S(2)}) collective-permute-start(bf16[1,4,4,32,256]{4,3,2,1,0:T(8,128)(2,1)S(1)} %constant_dynamic-update-slice_fusion.46), channel_id=1, source_target_pairs={{0,64},{1,65},{16,80},{17,81},{32,96},{33,97},{48,112},{49,113},{6... | collective-permute-start | bytes 786440 | tf_op jit(solution)/shard_map/ppermute | solution.py:38
  119.7 28.1 %collective-permute-start.57 = (bf16[1,1,4,32,1024]{4,3,2,1,0:T(8,128)(2,1)S(1)}, bf16[1,1,4,32,1024]{4,3,2,1,0:T(8,128)(2,1)S(1)}, u32[]{:S(2)}, u32[]{:S(2)}) collective-permute-start(bf16[1,1,4,32,1024]{4,3,2,1,0:T(8,128)(2,1)S(1)} %constant_dynamic-update-slice_fusion.26), channel_id=1, source_target_pairs={{0,2},{1,3},{16,18},{17,19},{32,34},{33,35},{48,50},{49,51},{64,66... | collective-permute-start | bytes 786440 | tf_op jit(solution)/shard_map/ppermute | solution.py:38
  125.0 23.5 %collective-permute-start.58 = (bf16[1,1,4,32,1024]{4,3,2,1,0:T(8,128)(2,1)S(1)}, bf16[1,1,4,32,1024]{4,3,2,1,0:T(8,128)(2,1)S(1)}, u32[]{:S(2)}, u32[]{:S(2)}) collective-permute-start(bf16[1,1,4,32,1024]{4,3,2,1,0:T(8,128)(2,1)S(1)} %constant_dynamic-update-slice_fusion.26), channel_id=1, source_target_pairs={{0,66},{1,67},{16,82},{17,83},{32,98},{33,99},{48,114},{49,115},{6... | collective-permute-start | bytes 786440 | tf_op jit(solution)/shard_map/ppermute | solution.py:38
  145.1 49.3 %collective-permute-start.50 = (bf16[4,4,1,32,1024]{4,3,2,1,0:T(8,128)(2,1)S(1)}, bf16[4,4,1,32,1024]{4,3,2,1,0:T(8,128)(2,1)S(1)}, u32[]{:S(2)}, u32[]{:S(2)}) collective-permute-start(bf16[4,4,1,32,1024]{4,3,2,1,0:T(8,128)(2,1)S(1)} %constant_dynamic-update-slice_fusion.34), channel_id=1, source_target_pairs={{0,4},{4,8},{8,12},{12,0},{1,5},{5,9},{9,13},{13,1},{2,6},{6,10},{... | collective-permute-start | bytes 3145736 | tf_op jit(solution)/shard_map/ppermute | solution.py:38
  145.2 51.0 %collective-permute-start.51 = (bf16[4,4,1,32,1024]{4,3,2,1,0:T(8,128)(2,1)S(1)}, bf16[4,4,1,32,1024]{4,3,2,1,0:T(8,128)(2,1)S(1)}, u32[]{:S(2)}, u32[]{:S(2)}) collective-permute-start(bf16[4,4,1,32,1024]{4,3,2,1,0:T(8,128)(2,1)S(1)} %constant_dynamic-update-slice_fusion.34), channel_id=1, source_target_pairs={{0,8},{4,12},{8,0},{12,4},{1,9},{5,13},{9,1},{13,5},{2,10},{6,14},... | collective-permute-start | bytes 3145736 | tf_op jit(solution)/shard_map/ppermute | solution.py:38
  147.8 48.4 %collective-permute-start.52 = (bf16[4,4,1,32,1024]{4,3,2,1,0:T(8,128)(2,1)S(1)}, bf16[4,4,1,32,1024]{4,3,2,1,0:T(8,128)(2,1)S(1)}, u32[]{:S(2)}, u32[]{:S(2)}) collective-permute-start(bf16[4,4,1,32,1024]{4,3,2,1,0:T(8,128)(2,1)S(1)} %constant_dynamic-update-slice_fusion.34), channel_id=1, source_target_pairs={{0,12},{4,0},{8,4},{12,8},{1,13},{5,1},{9,5},{13,9},{2,14},{6,2},{... | collective-permute-start | bytes 3145736 | tf_op jit(solution)/shard_map/ppermute | solution.py:38
  148.6 48.7 %collective-permute-start.59 = (bf16[4,1,4,32,1024]{4,3,2,1,0:T(8,128)(2,1)S(1)}, bf16[4,1,4,32,1024]{4,3,2,1,0:T(8,128)(2,1)S(1)}, u32[]{:S(2)}, u32[]{:S(2)}) collective-permute-start(bf16[4,1,4,32,1024]{4,3,2,1,0:T(8,128)(2,1)S(1)} %constant_dynamic-update-slice_fusion.22), channel_id=1, source_target_pairs={{0,16},{16,32},{32,48},{48,0},{64,80},{80,96},{96,112},{112,64},{1... | collective-permute-start | bytes 3145736 | tf_op jit(solution)/shard_map/ppermute | solution.py:38
  151.1 46.4 %collective-permute-start.60 = (bf16[4,1,4,32,1024]{4,3,2,1,0:T(8,128)(2,1)S(1)}, bf16[4,1,4,32,1024]{4,3,2,1,0:T(8,128)(2,1)S(1)}, u32[]{:S(2)}, u32[]{:S(2)}) collective-permute-start(bf16[4,1,4,32,1024]{4,3,2,1,0:T(8,128)(2,1)S(1)} %constant_dynamic-update-slice_fusion.22), channel_id=1, source_target_pairs={{0,32},{16,48},{32,0},{48,16},{64,96},{80,112},{96,64},{112,80},{1... | collective-permute-start | bytes 3145736 | tf_op jit(solution)/shard_map/ppermute | solution.py:38
  194.4 24.9 %collective-permute-start.61 = (bf16[4,1,4,32,1024]{4,3,2,1,0:T(8,128)(2,1)S(1)}, bf16[4,1,4,32,1024]{4,3,2,1,0:T(8,128)(2,1)S(1)}, u32[]{:S(2)}, u32[]{:S(2)}) collective-permute-start(bf16[4,1,4,32,1024]{4,3,2,1,0:T(8,128)(2,1)S(1)} %constant_dynamic-update-slice_fusion.22), channel_id=1, source_target_pairs={{0,48},{16,0},{32,16},{48,32},{64,112},{80,64},{96,80},{112,96},{1... | collective-permute-start | bytes 3145736 | tf_op jit(solution)/shard_map/ppermute | solution.py:38
  235.9 91.3 %collective-permute-start.122 = (bf16[4,4,1,32,1024]{4,3,2,1,0:T(8,128)(2,1)}, bf16[4,4,1,32,1024]{4,3,2,1,0:T(8,128)(2,1)S(1)}, u32[]{:S(2)}, u32[]{:S(2)}) collective-permute-start(bf16[4,4,1,32,1024]{4,3,2,1,0:T(8,128)(2,1)} %get-tuple-element.58), channel_id=1, source_target_pairs={{0,12},{4,0},{8,4},{12,8},{1,13},{5,1},{9,5},{13,9},{2,14},{6,2},{... | collective-permute-start | bytes 3145736 | tf_op jit(solution)/shard_map/ppermute | solution.py:38
  244.6 14.1 %collective-permute-start.113 = (bf16[1,4,4,32,256]{4,3,2,1,0:T(8,128)(2,1)S(1)}, bf16[1,4,4,32,256]{4,3,2,1,0:T(8,128)(2,1)S(1)}, u32[]{:S(2)}, u32[]{:S(2)}) collective-permute-start(bf16[1,4,4,32,256]{4,3,2,1,0:T(8,128)(2,1)S(1)} %get-tuple-element.101), channel_id=1, source_target_pairs={{0,66},{1,67},{16,82},{17,83},{32,98},{33,99},{48,114},{49,115},{6... | collective-permute-start | bytes 786440 | tf_op jit(solution)/shard_map/ppermute | solution.py:38
  247.3 13.5 %collective-permute-start.112 = (bf16[1,4,4,32,256]{4,3,2,1,0:T(8,128)(2,1)S(1)}, bf16[1,4,4,32,256]{4,3,2,1,0:T(8,128)(2,1)S(1)}, u32[]{:S(2)}, u32[]{:S(2)}) collective-permute-start(bf16[1,4,4,32,256]{4,3,2,1,0:T(8,128)(2,1)S(1)} %get-tuple-element.102), channel_id=1, source_target_pairs={{0,2},{1,3},{16,18},{17,19},{32,34},{33,35},{48,50},{49,51},{64,66... | collective-permute-start | bytes 786440 | tf_op jit(solution)/shard_map/ppermute | solution.py:38
  248.7 13.7 %collective-permute-start.111 = (bf16[1,4,4,32,256]{4,3,2,1,0:T(8,128)(2,1)S(1)}, bf16[1,4,4,32,256]{4,3,2,1,0:T(8,128)(2,1)S(1)}, u32[]{:S(2)}, u32[]{:S(2)}) collective-permute-start(bf16[1,4,4,32,256]{4,3,2,1,0:T(8,128)(2,1)S(1)} %get-tuple-element.100), channel_id=1, source_target_pairs={{0,64},{1,65},{16,80},{17,81},{32,96},{33,97},{48,112},{49,113},{6... | collective-permute-start | bytes 786440 | tf_op jit(solution)/shard_map/ppermute | solution.py:38
  254.7 87.5 %collective-permute-start.121 = (bf16[4,4,1,32,1024]{4,3,2,1,0:T(8,128)(2,1)}, bf16[4,4,1,32,1024]{4,3,2,1,0:T(8,128)(2,1)}, u32[]{:S(2)}, u32[]{:S(2)}) collective-permute-start(bf16[4,4,1,32,1024]{4,3,2,1,0:T(8,128)(2,1)} %get-tuple-element.59), channel_id=1, source_target_pairs={{0,8},{4,12},{8,0},{12,4},{1,9},{5,13},{9,1},{13,5},{2,10},{6,14},... | collective-permute-start | bytes 3145736 | tf_op jit(solution)/shard_map/ppermute | solution.py:38
  258.7 86.0 %collective-permute-start.120 = (bf16[4,4,1,32,1024]{4,3,2,1,0:T(8,128)(2,1)S(1)}, bf16[4,4,1,32,1024]{4,3,2,1,0:T(8,128)(2,1)}, u32[]{:S(2)}, u32[]{:S(2)}) collective-permute-start(bf16[4,4,1,32,1024]{4,3,2,1,0:T(8,128)(2,1)S(1)} %get-tuple-element.57), channel_id=1, source_target_pairs={{0,4},{4,8},{8,12},{12,0},{1,5},{5,9},{9,13},{13,1},{2,6},{6,10},{... | collective-permute-start | bytes 3145736 | tf_op jit(solution)/shard_map/ppermute | solution.py:38
  260.9 43.6 %collective-permute-start.67 = (bf16[1,344,128]{2,1,0:T(8,128)(2,1)S(1)}, bf16[1,344,128]{2,1,0:T(8,128)(2,1)S(1)}, u32[]{:S(2)}, u32[]{:S(2)}) collective-permute-start(bf16[1,344,128]{2,1,0:T(8,128)(2,1)S(1)} %get-tuple-element.119), channel_id=1, source_target_pairs={{0,8},{4,12},{8,0},{12,4},{1,9},{5,13},{9,1},{13,5},{2,10},{6,14},... | collective-permute-start | bytes 264200 | tf_op jit(solution)/shard_map/ppermute | solution.py:38
  262.4 44.8 %collective-permute-start.68 = (bf16[1,344,128]{2,1,0:T(8,128)(2,1)S(1)}, bf16[1,344,128]{2,1,0:T(8,128)(2,1)S(1)}, u32[]{:S(2)}, u32[]{:S(2)}) collective-permute-start(bf16[1,344,128]{2,1,0:T(8,128)(2,1)S(1)} %get-tuple-element.118), channel_id=1, source_target_pairs={{0,12},{4,0},{8,4},{12,8},{1,13},{5,1},{9,5},{13,9},{2,14},{6,2},{... | collective-permute-start | bytes 264200 | tf_op jit(solution)/shard_map/ppermute | solution.py:38
  309.7 17.5 %collective-permute-start.114 = (bf16[1,1,4,32,256]{4,3,2,1,0:T(8,128)(2,1)S(1)}, bf16[1,1,4,32,256]{4,3,2,1,0:T(8,128)(2,1)S(1)}, u32[]{:S(2)}, u32[]{:S(2)}) collective-permute-start(bf16[1,1,4,32,256]{4,3,2,1,0:T(8,128)(2,1)S(1)} %get-tuple-element.136), channel_id=1, source_target_pairs={{0,16},{16,32},{32,48},{48,0},{64,80},{80,96},{96,112},{112,64},{1... | collective-permute-start | bytes 196616 | tf_op jit(solution)/shard_map/ppermute | solution.py:38
  313.1 34.1 %collective-permute-start.131 = (bf16[4,1,4,32,1024]{4,3,2,1,0:T(8,128)(2,1)S(1)}, bf16[4,1,4,32,1024]{4,3,2,1,0:T(8,128)(2,1)}, u32[]{:S(2)}, u32[]{:S(2)}) collective-permute-start(bf16[4,1,4,32,1024]{4,3,2,1,0:T(8,128)(2,1)S(1)} %get-tuple-element.55), channel_id=1, source_target_pairs={{0,48},{16,0},{32,16},{48,32},{64,112},{80,64},{96,80},{112,96},{1... | collective-permute-start | bytes 3145736 | tf_op jit(solution)/shard_map/ppermute | solution.py:38
  327.2 23.2 %collective-permute-start.130 = (bf16[4,1,4,32,1024]{4,3,2,1,0:T(8,128)(2,1)S(1)}, bf16[4,1,4,32,1024]{4,3,2,1,0:T(8,128)(2,1)}, u32[]{:S(2)}, u32[]{:S(2)}) collective-permute-start(bf16[4,1,4,32,1024]{4,3,2,1,0:T(8,128)(2,1)S(1)} %get-tuple-element.56), channel_id=1, source_target_pairs={{0,32},{16,48},{32,0},{48,16},{64,96},{80,112},{96,64},{112,80},{1... | collective-permute-start | bytes 3145736 | tf_op jit(solution)/shard_map/ppermute | solution.py:38
  327.2 33.4 %collective-permute-start.129 = (bf16[4,1,4,32,1024]{4,3,2,1,0:T(8,128)(2,1)S(1)}, bf16[4,1,4,32,1024]{4,3,2,1,0:T(8,128)(2,1)}, u32[]{:S(2)}, u32[]{:S(2)}) collective-permute-start(bf16[4,1,4,32,1024]{4,3,2,1,0:T(8,128)(2,1)S(1)} %get-tuple-element.54), channel_id=1, source_target_pairs={{0,16},{16,32},{32,48},{48,0},{64,80},{80,96},{96,112},{112,64},{1... | collective-permute-start | bytes 3145736 | tf_op jit(solution)/shard_map/ppermute | solution.py:38
  342.2 38.3 %collective-permute-start.63 = (bf16[172,1024]{1,0:T(8,128)(2,1)S(1)}, bf16[172,1024]{1,0:T(8,128)(2,1)S(1)}, u32[]{:S(2)}, u32[]{:S(2)}) collective-permute-start(bf16[172,1024]{1,0:T(8,128)(2,1)S(1)} %constant_dynamic-slice_fusion.65), channel_id=1, source_target_pairs={{0,2},{1,3},{2,0},{3,1},{4,6},{5,7},{6,4},{7,5},{8,10},{9,11},{10,... | collective-permute-start | bytes 1056776 | tf_op jit(solution)/shard_map/ppermute | solution.py:42
  344.7 25.8 %collective-permute-start.69 = (bf16[1,3,344,128]{3,2,0,1:T(8,128)(2,1)S(1)}, bf16[1,3,344,128]{3,2,0,1:T(8,128)(2,1)S(1)}, u32[]{:S(2)}, u32[]{:S(2)}) collective-permute-start(bf16[1,3,344,128]{3,2,0,1:T(8,128)(2,1)S(1)} %get-tuple-element.86), channel_id=1, source_target_pairs={{0,4},{4,8},{8,12},{12,0},{1,5},{5,9},{9,13},{13,1},{2,6},{6,10},{... | collective-permute-start | bytes 792584 | tf_op jit(solution)/shard_map/ppermute | solution.py:38
  347.1 16.3 %collective-permute-start.119 = (bf16[1,1,1,32,256]{4,3,2,1,0:T(8,128)(2,1)S(1)}, bf16[1,1,1,32,256]{4,3,2,1,0:T(8,128)(2,1)S(1)}, u32[]{:S(2)}, u32[]{:S(2)}) collective-permute-start(bf16[1,1,1,32,256]{4,3,2,1,0:T(8,128)(2,1)S(1)} %get-tuple-element.165), channel_id=1, source_target_pairs={{0,12},{4,0},{8,4},{12,8},{1,13},{5,1},{9,5},{13,9},{2,14},{6,2},{... | collective-permute-start | bytes 49160 | tf_op jit(solution)/shard_map/ppermute | solution.py:38
  350.5 13.6 %collective-permute-start.118 = (bf16[1,1,1,32,256]{4,3,2,1,0:T(8,128)(2,1)S(1)}, bf16[1,1,1,32,256]{4,3,2,1,0:T(8,128)(2,1)S(1)}, u32[]{:S(2)}, u32[]{:S(2)}) collective-permute-start(bf16[1,1,1,32,256]{4,3,2,1,0:T(8,128)(2,1)S(1)} %get-tuple-element.166), channel_id=1, source_target_pairs={{0,8},{4,12},{8,0},{12,4},{1,9},{5,13},{9,1},{13,5},{2,10},{6,14},... | collective-permute-start | bytes 49160 | tf_op jit(solution)/shard_map/ppermute | solution.py:38
  366.9 14.9 %collective-permute-start.125 = (bf16[1,4,1,32,1024]{4,3,2,1,0:T(8,128)(2,1)S(1)}, bf16[1,4,1,32,1024]{4,3,2,1,0:T(8,128)(2,1)S(1)}, u32[]{:S(2)}, u32[]{:S(2)}) collective-permute-start(bf16[1,4,1,32,1024]{4,3,2,1,0:T(8,128)(2,1)S(1)} %get-tuple-element.98), channel_id=1, source_target_pairs={{0,66},{1,67},{16,82},{17,83},{32,98},{33,99},{48,114},{49,115},{6... | collective-permute-start | bytes 786440 | tf_op jit(solution)/shard_map/ppermute | solution.py:38
  371.5 16.7 %collective-permute-start.123 = (bf16[1,4,1,32,1024]{4,3,2,1,0:T(8,128)(2,1)S(1)}, bf16[1,4,1,32,1024]{4,3,2,1,0:T(8,128)(2,1)S(1)}, u32[]{:S(2)}, u32[]{:S(2)}) collective-permute-start(bf16[1,4,1,32,1024]{4,3,2,1,0:T(8,128)(2,1)S(1)} %get-tuple-element.97), channel_id=1, source_target_pairs={{0,64},{1,65},{16,80},{17,81},{32,96},{33,97},{48,112},{49,113},{6... | collective-permute-start | bytes 786440 | tf_op jit(solution)/shard_map/ppermute | solution.py:38
  374.9 13.4 %collective-permute-start.134 = (bf16[1,1,4,32,1024]{4,3,2,1,0:T(8,128)(2,1)S(1)}, bf16[1,1,4,32,1024]{4,3,2,1,0:T(8,128)(2,1)S(1)}, u32[]{:S(2)}, u32[]{:S(2)}) collective-permute-start(bf16[1,1,4,32,1024]{4,3,2,1,0:T(8,128)(2,1)S(1)} %get-tuple-element.95), channel_id=1, source_target_pairs={{0,66},{1,67},{16,82},{17,83},{32,98},{33,99},{48,114},{49,115},{6... | collective-permute-start | bytes 786440 | tf_op jit(solution)/shard_map/ppermute | solution.py:38
  381.8 24.7 %collective-permute-start.72 = (bf16[344,1024]{1,0:T(8,128)(2,1)S(1)}, bf16[344,1024]{1,0:T(8,128)(2,1)S(1)}, u32[]{:S(2)}, u32[]{:S(2)}) collective-permute-start(bf16[344,1024]{1,0:T(8,128)(2,1)S(1)} %fusion.38), channel_id=1, source_target_pairs={{0,1},{1,0},{2,3},{3,2},{4,5},{5,4},{6,7},{7,6},{8,9},{9,8},{10,11... | collective-permute-start | bytes 2113544 | tf_op jit(solution)/shard_map/ppermute | solution.py:42
  388.1 16.7 %collective-permute-start.64 = (bf16[172,1024]{1,0:T(8,128)(2,1)S(1)}, bf16[172,1024]{1,0:T(8,128)(2,1)S(1)}, u32[]{:S(2)}, u32[]{:S(2)}) collective-permute-start(bf16[172,1024]{1,0:T(8,128)(2,1)S(1)} %collective-permute-done.63), channel_id=1, source_target_pairs={{0,1},{1,0},{2,3},{3,2},{4,5},{5,4},{6,7},{7,6},{8,9},{9,8},{10,11... | collective-permute-start | bytes 1056776 | tf_op jit(solution)/shard_map/ppermute | solution.py:42
  407.7 12.6 %collective-permute-start.76 = (f32[1,88,128]{2,1,0:T(8,128)S(1)}, f32[1,88,128]{2,1,0:T(8,128)S(1)}, u32[]{:S(2)}, u32[]{:S(2)}) collective-permute-start(f32[1,88,128]{2,1,0:T(8,128)S(1)} %bitcast.411), channel_id=1, source_target_pairs={{0,8},{4,12},{8,0},{12,4},{1,9},{5,13},{9,1},{13,5},{2,10},{6,14},... | collective-permute-start | bytes 135176 | tf_op jit(solution)/shard_map/ppermute | solution.py:38
  415.2 87.0 %collective-permute-start.73 = (bf16[172,1024]{1,0:T(8,128)(2,1)S(1)}, bf16[172,1024]{1,0:T(8,128)(2,1)}, u32[]{:S(2)}, u32[]{:S(2)}) collective-permute-start(bf16[172,1024]{1,0:T(8,128)(2,1)S(1)} %constant_dynamic-slice_fusion.58), channel_id=1, source_target_pairs={{0,2},{1,3},{2,0},{3,1},{4,6},{5,7},{6,4},{7,5},{8,10},{9,11},{10,... | collective-permute-start | bytes 1056776 | tf_op jit(solution)/shard_map/ppermute | solution.py:42
  416.9 46.7 %collective-permute-start.104 = (bf16[4,1,4,32,256]{4,3,2,1,0:T(8,128)(2,1)}, bf16[4,1,4,32,256]{4,3,2,1,0:T(8,128)(2,1)}, u32[]{:S(2)}, u32[]{:S(2)}) collective-permute-start(bf16[4,1,4,32,256]{4,3,2,1,0:T(8,128)(2,1)} %get-tuple-element.110), channel_id=1, source_target_pairs={{0,48},{16,0},{32,16},{48,32},{64,112},{80,64},{96,80},{112,96},{1... | collective-permute-start | bytes 786440 | tf_op jit(solution)/shard_map/ppermute | solution.py:38
  419.4 44.2 %collective-permute-start.103 = (bf16[4,1,4,32,256]{4,3,2,1,0:T(8,128)(2,1)}, bf16[4,1,4,32,256]{4,3,2,1,0:T(8,128)(2,1)}, u32[]{:S(2)}, u32[]{:S(2)}) collective-permute-start(bf16[4,1,4,32,256]{4,3,2,1,0:T(8,128)(2,1)} %get-tuple-element.111), channel_id=1, source_target_pairs={{0,32},{16,48},{32,0},{48,16},{64,96},{80,112},{96,64},{112,80},{1... | collective-permute-start | bytes 786440 | tf_op jit(solution)/shard_map/ppermute | solution.py:38
  420.3 44.2 %collective-permute-start.102 = (bf16[4,1,4,32,256]{4,3,2,1,0:T(8,128)(2,1)}, bf16[4,1,4,32,256]{4,3,2,1,0:T(8,128)(2,1)}, u32[]{:S(2)}, u32[]{:S(2)}) collective-permute-start(bf16[4,1,4,32,256]{4,3,2,1,0:T(8,128)(2,1)} %get-tuple-element.109), channel_id=1, source_target_pairs={{0,16},{16,32},{32,48},{48,0},{64,80},{80,96},{96,112},{112,64},{1... | collective-permute-start | bytes 786440 | tf_op jit(solution)/shard_map/ppermute | solution.py:38
  (110 other events, 817.6 us)
